TPU v7x, 256 devices: a whole 4x4x8 slice. The times are simulated.
256 devices in a mesh: seq: 32 (over y, z), head: 8 (over x, core).
Axes of the slice: x: 4, y: 4, z: 8, core: 2. Of those that a mesh axis runs over, the one named last changes fastest.
Arguments:
- tokens: bfloat16 [32768, 4096], P('seq'), may hold values from -50 to 50
- norm_gain: float32 [4096], replicated, may hold values from 0.1 to 1.9
- wq: bfloat16 [4096, 4096], P('seq', 'head'), may hold values from -2.34375 to 2.34375
- wk: bfloat16 [4096, 1024], P('seq', 'head'), may hold values from -0.09375 to 0.09375
- wv: bfloat16 [4096, 1024], P('seq', 'head'), may hold values from -0.09375 to 0.09375
- wo: bfloat16 [4096, 4096], P('head', 'seq'), may hold values from -0.1875 to 0.1875
- gate_bias: float32 [32], P('head'), may hold values from -3 to 3
- mem_init: float32 [8, 128, 128], P('head'), may hold values from -32768 to 32768
- norm_init: float32 [8, 128], P('head'), may hold values from 512 to 2048
Outputs:
- attended: bfloat16 [32768, 4096], P('seq', 'head')
All inputs are finite; a program needn't handle non-finite values.
Results may differ from a plain program's by a relative error of at most 0.018.
Values may be sent and summed in bfloat16 or wider, within the bound.
No kernel may reach another device: no remote copies, remote signals or barrier semaphores. Data moves between devices by JAX's collectives and lax.ppermute only.
A program may use at most 128 MiB of HBM per device.

v0:
```python
import functools
import math

import jax
import jax.numpy as jnp
from jax import lax
from jax.experimental import pallas as pl
from jax.experimental.pallas import tpu as pltpu
from jax.sharding import PartitionSpec as P

HD = 128
SEG = 512
NY, NZ, NX = 4, 8, 4
SEQ = NY * NZ
HEADS = 2 * NX
F32 = jnp.float32
BF16 = jnp.bfloat16
VMEM_LIMIT = 20 << 20
VMEM_MOST = 32 << 20


def z_move(block, distance):
    return lax.ppermute(
        block, "seq", [(y * NZ + z, y * NZ + (z + distance) % NZ) for y in range(NY) for z in range(NZ)]
    )


def z_swap(block, bit):
    return lax.ppermute(block, "seq", [(s, s ^ bit) for s in range(SEQ)])


def y_move(block, distance):
    return lax.ppermute(
        block, "seq", [(y * NZ + z, (y + distance) % NY * NZ + z) for y in range(NY) for z in range(NZ)]
    )


def z_gather(block):
    return lax.all_gather(block, "seq", axis=0, axis_index_groups=[[y * NZ + z for z in range(NZ)] for y in range(NY)])


def x_move(block, distance):
    return lax.ppermute(
        block, "head", [(2 * x + c, 2 * ((x + distance) % NX) + c) for x in range(NX) for c in range(2)]
    )


def core_swap(block):
    return lax.ppermute(block, "head", [(h, h ^ 1) for h in range(HEADS)])


def spread_wo(block):
    pairs = []
    for y in range(NY):
        for z in range(NZ):
            for h in range(HEADS):
                pairs.append(((4 * h + y) * HEADS + z, (y * NZ + z) * HEADS + h))
    return lax.ppermute(block, ("seq", "head"), pairs)


def feature_map(values_in):
    return jnp.where(values_in > 0, values_in + 1.0, jnp.exp(jnp.minimum(values_in, 0.0)))


def split(wide):
    high = wide.astype(BF16)
    return high, (wide - high.astype(F32)).astype(BF16)


def norm_kernel(order, x_ref, gain_ref, out_ref):
    wide = x_ref[...].astype(F32)
    scale = lax.rsqrt(jnp.mean(wide * wide, axis=-1, keepdims=True) + 1e-05)
    for block in range(SEQ):
        at = pl.ds(pl.multiple_of(order[block] * HD, HD), HD)
        part = x_ref[:, at].astype(F32) * scale * gain_ref[:, at]
        out_ref[:, block * HD : (block + 1) * HD] = part.astype(BF16)


def norm_call(tokens, gain, order):
    rows, width = tokens.shape
    tile = 128
    return pl.pallas_call(
        norm_kernel,
        out_shape=jax.ShapeDtypeStruct((rows, width), BF16),
        grid_spec=pltpu.PrefetchScalarGridSpec(
            num_scalar_prefetch=1,
            grid=(rows // tile,),
            in_specs=[
                pl.BlockSpec((tile, width), lambda i, o: (i, 0)),
                pl.BlockSpec((1, width), lambda i, o: (0, 0)),
            ],
            out_specs=pl.BlockSpec((tile, width), lambda i, o: (i, 0)),
        ),
        cost_estimate=pl.CostEstimate(flops=6 * rows * width, bytes_accessed=4 * rows * width, transcendentals=rows),
        name="norm",
    )(order, tokens, gain.reshape(1, width))


def fetch(sources, targets, sems):
    copies = [pltpu.make_async_copy(s, t, sems.at[n]) for n, (s, t) in enumerate(zip(sources, targets))]

    @pl.when(pl.program_id(0) == 0)
    def _():
        for copy in copies:
            copy.start()

    return copies


def arrived(copy):
    @pl.when(pl.program_id(0) == 0)
    def _():
        copy.wait()


COLUMNS = 4


def column_blocks(tile, width):
    return [pl.BlockSpec((tile, width // COLUMNS), lambda i, n=n: (i, n)) for n in range(COLUMNS)]


def q_kernel(*refs):
    x_refs, (w_ref, q_ref, held, sems) = refs[:COLUMNS], refs[COLUMNS:]
    size = SEQ // COLUMNS
    parts = [pl.ds(n * size, size) for n in range(COLUMNS)]
    copies = fetch([w_ref.at[part] for part in parts], [held.at[part] for part in parts], sems)
    wide = None
    for n, (copy, x_ref) in enumerate(zip(copies, x_refs)):
        arrived(copy)
        weight = held[n * size : (n + 1) * size].reshape(size * HD, 4 * HD)
        term = jnp.dot(x_ref[...], weight, preferred_element_type=F32)
        wide = term if wide is None else wide + term
    q_ref[...] = wide.astype(BF16)


def q_call(normed, weight):
    rows, width = normed.shape
    tile = 256
    return pl.pallas_call(
        q_kernel,
        grid=(rows // tile,),
        out_shape=jax.ShapeDtypeStruct((rows, 4 * HD), BF16),
        in_specs=[*column_blocks(tile, width), pl.BlockSpec(memory_space=pltpu.HBM)],
        out_specs=pl.BlockSpec((tile, 4 * HD), lambda i: (i, 0)),
        scratch_shapes=[pltpu.VMEM((SEQ, HD, 4 * HD), BF16), pltpu.SemaphoreType.DMA((COLUMNS,))],
        cost_estimate=pl.CostEstimate(flops=2 * rows * width * 4 * HD, bytes_accessed=12 << 20, transcendentals=0),
        compiler_params=pltpu.CompilerParams(vmem_limit_bytes=56 << 20),
        name="q",
    )(*[normed] * COLUMNS, weight)


def kv_kernel(*refs):
    x_refs, pieces = refs[:COLUMNS], refs[COLUMNS : COLUMNS + NY]
    k_ref, v_ref, delta_ref, held, sems = refs[COLUMNS + NY :]
    copies = fetch([piece.at[pl.ds(0, NZ)] for piece in pieces], [held.at[:, e] for e in range(NY)], sems)
    for copy in copies:
        arrived(copy)
    each = NZ // COLUMNS
    wide = None
    for n, x_ref in enumerate(x_refs):
        weight = held[n * each : (n + 1) * each].reshape(each * NY * HD, 2 * HD)
        term = jnp.dot(x_ref[...], weight, preferred_element_type=F32)
        wide = term if wide is None else wide + term
    keys = wide[:, :HD].astype(BF16)
    values = wide[:, HD:].astype(BF16)
    k_ref[...] = keys
    v_ref[...] = values
    feats = feature_map(keys.astype(F32))
    high, low = split(feats)
    by_rows = (((0,), (0,)), ((), ()))
    memory = lax.dot_general(high, values, by_rows, preferred_element_type=F32)
    memory += lax.dot_general(low, values, by_rows, preferred_element_type=F32)
    norm = jnp.broadcast_to(jnp.sum(feats, axis=0, keepdims=True), (8, HD))

    @pl.when(pl.program_id(0) % 2 == 0)
    def _():
        delta_ref[0, :HD, :] = memory
        delta_ref[0, HD:, :] = norm

    @pl.when(pl.program_id(0) % 2 == 1)
    def _():
        delta_ref[0, :HD, :] += memory
        delta_ref[0, HD:, :] += norm


def kv_call(normed, pieces):
    rows, width = normed.shape
    tile = SEG // 2
    row_block = pl.BlockSpec((tile, HD), lambda i: (i, 0))
    return pl.pallas_call(
        kv_kernel,
        grid=(rows // tile,),
        out_shape=[
            jax.ShapeDtypeStruct((rows, HD), BF16),
            jax.ShapeDtypeStruct((rows, HD), BF16),
            jax.ShapeDtypeStruct((rows // SEG, HD + 8, HD), F32),
        ],
        in_specs=[*column_blocks(tile, width), *[pl.BlockSpec(memory_space=pltpu.HBM)] * len(pieces)],
        out_specs=[row_block, row_block, pl.BlockSpec((1, HD + 8, HD), lambda i: (i // 2, 0, 0))],
        scratch_shapes=[pltpu.VMEM((NZ, NY, HD, 2 * HD), BF16), pltpu.SemaphoreType.DMA((NY,))],
        cost_estimate=pl.CostEstimate(flops=2 * rows * width * 2 * HD, bytes_accessed=10 << 20, transcendentals=rows * HD),
        compiler_params=pltpu.CompilerParams(vmem_limit_bytes=VMEM_MOST),
        name="kv",
    )(*[normed] * COLUMNS, *pieces)


def local_kernel(q_ref, k_ref, v_ref, out_ref):
    scale = 1.0 / math.sqrt(HD)
    half = SEG // 2
    transposed = (((1,), (1,)), ((), ()))
    for head in range(4):
        for part in range(2):
            rows = slice(part * half, (part + 1) * half)
            seen = (part + 1) * half
            query = q_ref[rows, head * HD : (head + 1) * HD]
            scores = lax.dot_general(query, k_ref[:seen, :], transposed, preferred_element_type=F32) * scale
            row = lax.broadcasted_iota(jnp.int32, (half, seen), 0) + part * half
            column = lax.broadcasted_iota(jnp.int32, (half, seen), 1)
            scores = jnp.where(row >= column, scores, -1e30)
            expd = jnp.exp(scores - jnp.max(scores, axis=-1, keepdims=True))
            probs = (expd / jnp.sum(expd, axis=-1, keepdims=True)).astype(BF16)
            out_ref[rows, head * HD : (head + 1) * HD] = jnp.dot(
                probs, v_ref[:seen, :], preferred_element_type=F32
            )


def local_call(queries, keys, values, segment):
    row_block = lambda n: pl.BlockSpec((SEG, n), lambda i: (segment, 0))
    return pl.pallas_call(
        local_kernel,
        grid=(1,),
        out_shape=jax.ShapeDtypeStruct((SEG, 4 * HD), F32),
        in_specs=[row_block(4 * HD), row_block(HD), row_block(HD)],
        out_specs=pl.BlockSpec((SEG, 4 * HD), lambda i: (0, 0)),
        cost_estimate=pl.CostEstimate(flops=16 * SEG * SEG * HD, bytes_accessed=2 << 20, transcendentals=4 * SEG * SEG),
        compiler_params=pltpu.CompilerParams(vmem_limit_bytes=VMEM_LIMIT),
        name="local",
    )(queries, keys, values)


def mix_kernel(gate_ref, q_ref, local_ref, memory_ref, out_ref):
    memory = memory_ref[:HD, :]
    normer = jnp.broadcast_to(memory_ref[HD : HD + 1, :], (HD, HD)).T
    both_high, both_low = split(jnp.concatenate([memory, normer], axis=1))
    for head in range(4):
        at = slice(head * HD, (head + 1) * HD)
        high, low = split(feature_map(q_ref[:, at].astype(F32)))
        both = jnp.dot(high, both_high, preferred_element_type=F32)
        both += jnp.dot(high, both_low, preferred_element_type=F32)
        both += jnp.dot(low, both_high, preferred_element_type=F32)
        gate = gate_ref[head]
        mixed = gate * (both[:, :HD] / both[:, HD:]) + (1.0 - gate) * local_ref[:, at]
        out_ref[:, at] = mixed.astype(BF16)


def mix_call(gate, queries, local, memory, segment):
    row_block = pl.BlockSpec((SEG, 4 * HD), lambda i: (segment, 0))
    return pl.pallas_call(
        mix_kernel,
        grid=(1,),
        out_shape=jax.ShapeDtypeStruct((SEG, 4 * HD), BF16),
        in_specs=[
            pl.BlockSpec(memory_space=pltpu.SMEM),
            row_block,
            pl.BlockSpec((SEG, 4 * HD), lambda i: (0, 0)),
            pl.BlockSpec((HD + 8, HD), lambda i: (0, 0)),
        ],
        out_specs=pl.BlockSpec((SEG, 4 * HD), lambda i: (0, 0)),
        cost_estimate=pl.CostEstimate(flops=48 * SEG * HD * HD, bytes_accessed=2 << 20, transcendentals=4 * SEG * HD),
        compiler_params=pltpu.CompilerParams(vmem_limit_bytes=16 << 20),
        name="mix",
    )(gate, queries, local, memory)


def out_kernel(count, order, *refs):
    mixed_refs, (w_hbm, out_ref, rest_ref, weights, sems) = refs[: 2 * count], refs[2 * count :]
    copies = []
    for p in range(count + 2):
        target = weights.at[p] if p < count else rest_ref.at[p - count]
        mine = [
            pltpu.make_async_copy(
                w_hbm.at[order[p], order[count + 2 + j], :, n * HD : (n + 1) * HD],
                target.at[n * 2 * HD : (n + 1) * 2 * HD, j * HD : (j + 1) * HD],
                sems.at[p, 2 * j + n],
            )
            for j in range(NY)
            for n in range(2)
        ]
        for copy in mine:
            copy.start()
        copies.append(mine)
    totals = [None, None]
    for p in range(count):
        for copy in copies[p]:
            copy.wait()
        for s in range(2):
            term = jnp.dot(mixed_refs[2 * p + s][...], weights[p], preferred_element_type=F32)
            totals[s] = term if totals[s] is None else totals[s] + term
    for s in range(2):
        out_ref[s * SEG : (s + 1) * SEG, :] = totals[s]
    for mine in copies[count:]:
        for copy in mine:
            copy.wait()


def out_call(order, pieces, weight):
    count = len(pieces)
    vmem = pl.BlockSpec(memory_space=pltpu.VMEM)
    return pl.pallas_call(
        functools.partial(out_kernel, count),
        out_shape=[
            jax.ShapeDtypeStruct((2 * SEG, 4 * HD), F32),
            jax.ShapeDtypeStruct((2, 4 * HD, 4 * HD), BF16),
        ],
        in_specs=[
            pl.BlockSpec(memory_space=pltpu.SMEM),
            *[vmem] * (2 * count),
            pl.BlockSpec(memory_space=pltpu.HBM),
        ],
        out_specs=[vmem, vmem],
        scratch_shapes=[
            pltpu.VMEM((count, 4 * HD, 4 * HD), BF16),
            pltpu.SemaphoreType.DMA((count + 2, 2 * NY)),
        ],
        cost_estimate=pl.CostEstimate(flops=4 * count * SEG * 16 * HD * HD, bytes_accessed=(2 * count + 4) << 20, transcendentals=0),
        compiler_params=pltpu.CompilerParams(vmem_limit_bytes=VMEM_LIMIT),
        name="out",
    )(order, *[part for piece in pieces for part in piece], weight)


def add_kernel(which, mixed_0, mixed_1, w_ref, so_far, out_ref):
    for s, mixed_ref in enumerate((mixed_0, mixed_1)):
        at = slice(s * SEG, (s + 1) * SEG)
        term = jnp.dot(mixed_ref[...], w_ref[which], preferred_element_type=F32)
        out_ref[at, :] = (so_far[at, :] + term).astype(out_ref.dtype)


def add_call(which, piece, weights, so_far, dtype):
    vmem = pl.BlockSpec(memory_space=pltpu.VMEM)
    return pl.pallas_call(
        functools.partial(add_kernel, which),
        out_shape=jax.ShapeDtypeStruct(so_far.shape, dtype),
        in_specs=[vmem] * 4,
        out_specs=vmem,
        cost_estimate=pl.CostEstimate(flops=4 * SEG * 16 * HD * HD, bytes_accessed=4 << 20, transcendentals=0),
        compiler_params=pltpu.CompilerParams(vmem_limit_bytes=VMEM_LIMIT),
        name="add",
    )(*piece, weights, so_far)


def per_device(tokens, norm_gain, wq, wk, wv, wo, gate_bias, mem_init, norm_init):
    seq, head = lax.axis_index("seq"), lax.axis_index("head")
    y, z = seq // NZ, seq % NZ
    x, core = head // 2, head % 2

    together = lax.optimization_barrier
    z_index, e_index = jnp.arange(SEQ) // NY, jnp.arange(SEQ) % NY
    order = ((y - e_index) % NY * NZ + z_index).astype(jnp.int32)

    wkv = jnp.concatenate([wk, wv], axis=1)
    wq_1, wq_2, wq_3 = y_move(wq, 1), y_move(wq, 2), y_move(wq, -1)
    one, back = z_move(wkv, 1), z_move(wkv, -1)
    wo_own = spread_wo(wo)
    wq_1, wq_2, wq_3, one, back, wo_own = together((wq_1, wq_2, wq_3, one, back, wo_own))
    wq_y = jnp.stack([wq, wq_1, wq_2, wq_3])
    trio = jnp.stack([back, wkv, one])
    wkv_p, wkv_m = z_move(trio, 3), z_move(trio[1:], -3)
    wq_y, wkv_p, wkv_m = together((wq_y, wkv_p, wkv_m))
    wq_gathered = z_gather(wq_y)
    wkv_z = jnp.concatenate(
        [wkv[None], back[None], wkv_m[1:], wkv_m[:1], wkv_p[2:], wkv_p[1:2], wkv_p[:1], one[None]]
    )
    wkv_z = lax.dynamic_slice_in_dim(jnp.concatenate([wkv_z, wkv_z[:-1]]), (NZ - z) % NZ, NZ)
    half = wo_own.shape[0] // 2
    wo_own = jnp.concatenate([wo_own[:half], wo_own[half:]], axis=1).reshape(2, HD, 2 * HD)
    packed = jnp.concatenate([wkv_z, wo_own])
    packs = [packed, y_move(packed, 1), y_move(packed, 2), y_move(packed, -1)]
    normed = norm_call(tokens, norm_gain, order)
    *packs, normed = together((*packs, normed))
    keys, values, delta = kv_call(normed, packs)
    wo_y = jnp.stack([pack[NZ:].reshape(half, 2 * HD) for pack in packs])
    wo_gathered = z_gather(wo_y)

    total = delta[0] + delta[1]
    before = jnp.concatenate([mem_init[0], jnp.broadcast_to(norm_init, (8, HD))], axis=0)
    for bit in (1, 2, 4):
        other = z_swap(total.astype(BF16), bit).astype(F32)
        before = before + jnp.where((z & bit) > 0, other, 0.0)
        total = total + other
    total, wq_gathered = together((total, wq_gathered))
    queries = q_call(normed, wq_gathered.reshape(SEQ, HD, 4 * HD))
    narrow = total.astype(BF16)
    for e, other in ((1, y_move(narrow, 1)), (2, y_move(narrow, 2)), (3, y_move(narrow, -1))):
        before = before + jnp.where(y >= e, other.astype(F32), 0.0)

    gate = jax.nn.sigmoid(gate_bias)
    local = [local_call(queries, keys, values, segment) for segment in range(2)]
    own = [
        mix_call(gate, queries, local[0], before, 0),
        mix_call(gate, queries, local[1], before + delta[0], 1),
    ]

    left = [x_move(own[0], 1)]
    right = [x_move(own[0], -1)]
    left.append(x_move(own[1], 1))
    right.append(x_move(own[1], -1))
    opposite = [x_move(left[0], 1), x_move(right[1], -1)]
    own_swapped = [core_swap(part) for part in own]

    def both(piece):
        return [piece, [core_swap(part) for part in piece]]

    def rows_of(distance):
        index = (x - distance) % NX * 2
        return [index + core, index + 1 - core]

    blocks = [(y - j) % NY for j in range(NY)]
    at = jnp.stack([row for d in (0, 1, -1, 2) for row in rows_of(d)] + blocks).astype(jnp.int32)
    near = [own, own_swapped, *both(left), *both(right)]
    so_far, rest = out_call(at, near, wo_gathered)
    opposite[0], opposite[1], so_far = together((opposite[0], opposite[1], so_far))
    swapped = [core_swap(part) for part in opposite]
    so_far = add_call(0, opposite, rest, so_far, F32)
    swapped[0], swapped[1], so_far = together((swapped[0], swapped[1], so_far))
    return add_call(1, swapped, rest, so_far, BF16)


def solution(mesh):
    placed = (
        P("seq", None),
        P(),
        P("seq", "head"),
        P("seq", "head"),
        P("seq", "head"),
        P("head", "seq"),
        P("head"),
        P("head", None, None),
        P("head", None),
    )
    return jax.shard_map(
        per_device, mesh=mesh, in_specs=placed, out_specs=P("seq", "head"), check_vma=False
    )
```

profile of v0, /device:TPU:1, one launch (start us, length us, event | category | flops | bytes accessed | tf_op | source)
XLA Modules:
  0.0 191.5 jit_solution(13753182571517806397)
XLA Ops:
  8.1 2.5 %collective-permute-start.3 = (bf16[128,256]{1,0:T(8,128)(2,1)S(1)}, bf16[128,256]{1,0:T(8,128)(2,1)S(1)}, u32[]{:S(2)}, u32[]{:S(2)}) collective-permute-start(bf16[128,256]{1,0:T(8,128)(2,1)S(1)} %constant_dynamic-update-slice_fusion), channel_id=1, source_target_pairs={{0,8},{8,16},{16,24},{24,32},{32,40},{40,48},{48,56},{56,0},{64,72... | collective-permute-start | bytes 196616 | tf_op jit(solution)/shard_map/ppermute | solution.py:23
  10.6 1.3 collective-permute-start
  11.9 2.6 %collective-permute-start.1 = (bf16[128,512]{1,0:T(8,128)(2,1)}, bf16[128,512]{1,0:T(8,128)(2,1)S(1)}, u32[]{:S(2)}, u32[]{:S(2)}) collective-permute-start(bf16[128,512]{1,0:T(8,128)(2,1)} %param.11), channel_id=1, source_target_pairs={{0,128},{8,136},{16,144},{24,152},{32,160},{40,168},{48,176},{56,1... | collective-permute-start | bytes 393224 | tf_op jit(solution)/shard_map/ppermute | solution.py:33
  14.5 1.1 collective-permute-start.2
  15.6 5.2 %collective-permute-start.5 = (bf16[512,128]{1,0:T(8,128)(2,1)}, bf16[512,128]{1,0:T(8,128)(2,1)S(1)}, u32[]{:S(2)}, u32[]{:S(2)}) collective-permute-start(bf16[512,128]{1,0:T(8,128)(2,1)} %param.14), channel_id=1, source_target_pairs={{0,0},{32,1},{64,2},{96,3},{128,4},{160,5},{192,6},{224,7},{1,8},{... | collective-permute-start | bytes 393224 | tf_op jit(solution)/shard_map/ppermute | solution.py:58
  21.6 3.7 %collective-permute-done.4 = bf16[128,256]{1,0:T(8,128)(2,1)S(1)} collective-permute-done((bf16[128,256]{1,0:T(8,128)(2,1)S(1)}, bf16[128,256]{1,0:T(8,128)(2,1)S(1)}, u32[]{:S(2)}, u32[]{:S(2)}) %collective-permute-start.4) | collective-permute-done | bytes 65568 | tf_op jit(solution)/shard_map/ppermute | solution.py:23
  25.4 2.9 %collective-permute-done.5 = bf16[512,128]{1,0:T(8,128)(2,1)S(1)} collective-permute-done((bf16[512,128]{1,0:T(8,128)(2,1)}, bf16[512,128]{1,0:T(8,128)(2,1)S(1)}, u32[]{:S(2)}, u32[]{:S(2)}) %collective-permute-start.5) | collective-permute-done | bytes 131104 | tf_op jit(solution)/shard_map/ppermute | solution.py:58
  28.3 8.3 %collective-permute-start.6 = (bf16[3,128,256]{2,1,0:T(8,128)(2,1)S(1)}, bf16[3,128,256]{2,1,0:T(8,128)(2,1)S(1)}, u32[]{:S(2)}, u32[]{:S(2)}) collective-permute-start(bf16[3,128,256]{2,1,0:T(8,128)(2,1)S(1)} %pad_maximum_fusion.3), channel_id=1, source_target_pairs={{0,24},{8,32},{16,40},{24,48},{32,56},{40,0},{48,8},{56,16},{64,88... | collective-permute-start | bytes 589832 | tf_op jit(solution)/shard_map/ppermute | solution.py:23
  36.7 1.8 pad_maximum_fusion.1
  38.4 4.2 %collective-permute-done.7 = bf16[2,128,256]{2,1,0:T(8,128)(2,1)S(1)} collective-permute-done((bf16[2,128,256]{2,1,0:T(8,128)(2,1)S(1)}, bf16[2,128,256]{2,1,0:T(8,128)(2,1)S(1)}, u32[]{:S(2)}, u32[]{:S(2)}) %collective-permute-start.7) | collective-permute-done | bytes 131104 | tf_op jit(solution)/shard_map/ppermute | solution.py:23
  42.7 6.0 %collective-permute-done.6 = bf16[3,128,256]{2,1,0:T(8,128)(2,1)S(1)} collective-permute-done((bf16[3,128,256]{2,1,0:T(8,128)(2,1)S(1)}, bf16[3,128,256]{2,1,0:T(8,128)(2,1)S(1)}, u32[]{:S(2)}, u32[]{:S(2)}) %collective-permute-start.6) | collective-permute-done | bytes 196640 | tf_op jit(solution)/shard_map/ppermute | solution.py:23
  49.2 2.6 %collective-permute-start.8 = (bf16[10,128,256]{2,1,0:T(8,128)(2,1)S(1)}, bf16[10,128,256]{2,1,0:T(8,128)(2,1)S(1)}, u32[]{:S(2)}, u32[]{:S(2)}) collective-permute-start(bf16[10,128,256]{2,1,0:T(8,128)(2,1)S(1)} %pad_maximum_fusion.refs_4_), channel_id=1, source_target_pairs={{0,64},{8,72},{16,80},{24,88},{32,96},{40,104},{48,112},{56,120},{... | collective-permute-start | bytes 1966088 | tf_op jit(solution)/shard_map/ppermute | solution.py:33
  51.8 2.5 %collective-permute-start.10 = (bf16[10,128,256]{2,1,0:T(8,128)(2,1)S(1)}, bf16[10,128,256]{2,1,0:T(8,128)(2,1)S(1)}, u32[]{:S(2)}, u32[]{:S(2)}) collective-permute-start(bf16[10,128,256]{2,1,0:T(8,128)(2,1)S(1)} %pad_maximum_fusion.refs_4_), channel_id=1, source_target_pairs={{0,192},{8,200},{16,208},{24,216},{32,224},{40,232},{48,240},{56,2... | collective-permute-start | bytes 1966088 | tf_op jit(solution)/shard_map/ppermute | solution.py:33
  54.9 11.4 %norm.1.refs_0_.refs_1_.refs_2_.refs_3_ = bf16[1024,4096]{1,0:T(8,128)(2,1)} custom-call(s32[32]{0:T(128)} %fusion.8.order, bf16[1024,4096]{1,0:T(8,128)(2,1)} %x_ref.1, f32[1,4096]{1,0:T(1,128)} %bitcast.58), custom_call_target="tpu_custom_call" | custom-call | flops 25165824 | bytes 16777216 | tf_op jit(solution)/shard_map/norm/pallas_call | solution.py:82
  66.3 12.9 %collective-permute-done.8.refs_5_ = bf16[10,128,256]{2,1,0:T(8,128)(2,1)S(1)} collective-permute-done((bf16[10,128,256]{2,1,0:T(8,128)(2,1)S(1)}, bf16[10,128,256]{2,1,0:T(8,128)(2,1)S(1)}, u32[]{:S(2)}, u32[]{:S(2)}) %collective-permute-start.8) | collective-permute-done | bytes 655392 | tf_op jit(solution)/shard_map/ppermute | solution.py:33
  79.4 1.4 collective-permute-done.10.refs_7_
  81.7 3.5 %copy-done = bf16[1024,4096]{1,0:T(8,128)(2,1)S(1)} copy-done((bf16[1024,4096]{1,0:T(8,128)(2,1)S(1)}, bf16[1024,4096]{1,0:T(8,128)(2,1)}, u32[]{:S(2)}) %copy-start) | copy-done | bytes 8388632
  85.2 4.9 %kv.1 = (bf16[1024,128]{1,0:T(8,128)(2,1)S(1)}, bf16[1024,128]{1,0:T(8,128)(2,1)S(1)}, f32[2,136,128]{2,1,0:T(8,128)S(1)}) custom-call(bf16[1024,4096]{1,0:T(8,128)(2,1)S(1)} %copy-done, bf16[1024,4096]{1,0:T(8,128)(2,1)S(1)} %copy-done, bf16[1024,4096]{1,0:T(8,128)(2,1)S(1)} %copy-done, bf16[1024,4096]{1,0:T(8,128)(2,1)S(1)} %copy-done, ...), custom_call_target="tpu_custom_call" | custom-call | flops 2147483648 | bytes 10485760 | tf_op jit(solution)/shard_map/kv/pallas_call | solution.py:191
  90.0 2.8 %collective-permute-start.11 = (bf16[136,128]{1,0:T(8,128)(2,1)S(1)}, bf16[136,128]{1,0:T(8,128)(2,1)S(1)}, u32[]{:S(2)}, u32[]{:S(2)}) collective-permute-start(bf16[136,128]{1,0:T(8,128)(2,1)S(1)} %get-tuple-element.61), channel_id=1, source_target_pairs={{0,8},{8,0},{16,24},{24,16},{32,40},{40,32},{48,56},{56,48},{64,72... | collective-permute-start | bytes 104456 | tf_op jit(solution)/shard_map/ppermute | solution.py:29
  92.9 2.4 %collective-permute-done.11 = bf16[136,128]{1,0:T(8,128)(2,1)S(1)} collective-permute-done((bf16[136,128]{1,0:T(8,128)(2,1)S(1)}, bf16[136,128]{1,0:T(8,128)(2,1)S(1)}, u32[]{:S(2)}, u32[]{:S(2)}) %collective-permute-start.11) | collective-permute-done | bytes 34848 | tf_op jit(solution)/shard_map/ppermute | solution.py:29
  95.3 1.5 collective-permute-start.12
  96.8 3.4 %collective-permute-done.12 = bf16[136,128]{1,0:T(8,128)(2,1)S(1)} collective-permute-done((bf16[136,128]{1,0:T(8,128)(2,1)S(1)}, bf16[136,128]{1,0:T(8,128)(2,1)S(1)}, u32[]{:S(2)}, u32[]{:S(2)}) %collective-permute-start.12) | collective-permute-done | bytes 34848 | tf_op jit(solution)/shard_map/ppermute | solution.py:29
  100.2 7.3 %collective-permute-start.13 = (bf16[136,128]{1,0:T(8,128)(2,1)S(1)}, bf16[136,128]{1,0:T(8,128)(2,1)S(1)}, u32[]{:S(2)}, u32[]{:S(2)}) collective-permute-start(bf16[136,128]{1,0:T(8,128)(2,1)S(1)} %fusion.7), channel_id=1, source_target_pairs={{0,32},{8,40},{16,48},{24,56},{32,0},{40,8},{48,16},{56,24},{64,96... | collective-permute-start | bytes 104456 | tf_op jit(solution)/shard_map/ppermute | solution.py:29
  107.5 2.0 %collective-permute-done.13 = bf16[136,128]{1,0:T(8,128)(2,1)S(1)} collective-permute-done((bf16[136,128]{1,0:T(8,128)(2,1)S(1)}, bf16[136,128]{1,0:T(8,128)(2,1)S(1)}, u32[]{:S(2)}, u32[]{:S(2)}) %collective-permute-start.13) | collective-permute-done | bytes 34848 | tf_op jit(solution)/shard_map/ppermute | solution.py:29
  109.6 2.4 %collective-permute-start.16 = (bf16[136,128]{1,0:T(8,128)(2,1)S(1)}, bf16[136,128]{1,0:T(8,128)(2,1)S(1)}, u32[]{:S(2)}, u32[]{:S(2)}) collective-permute-start(bf16[136,128]{1,0:T(8,128)(2,1)S(1)} %convert_add_fusion), channel_id=1, source_target_pairs={{0,192},{8,200},{16,208},{24,216},{32,224},{40,232},{48,240},{56,2... | collective-permute-start | bytes 104456 | tf_op jit(solution)/shard_map/ppermute | solution.py:33
  112.8 9.9 %q.1.q_ref = bf16[1024,512]{1,0:T(8,128)(2,1)} custom-call(bf16[1024,4096]{1,0:T(8,128)(2,1)} %norm.1.refs_0_.refs_1_.refs_2_.refs_3_, bf16[1024,4096]{1,0:T(8,128)(2,1)} %norm.1.refs_0_.refs_1_.refs_2_.refs_3_, bf16[1024,4096]{1,0:T(8,128)(2,1)} %norm.1.refs_0_.refs_1_.refs_2_.refs_3_, bf16[1024,4096]{1,0:T(8,128)(2,1)} %norm.1.refs_0_.refs_1_.refs_2_.refs_3_, ...), custom_call_target="tpu_custom_call" | custom-call | flops 4294967296 | bytes 12582912 | tf_op jit(solution)/shard_map/q/pallas_call | solution.py:140
  122.7 1.2 copy-done.1
  123.9 3.4 %local.2.local_ref = f32[512,512]{1,0:T(8,128)S(1)} custom-call(bf16[1024,512]{1,0:T(8,128)(2,1)S(1)} %copy-done.1, bf16[1024,128]{1,0:T(8,128)(2,1)S(1)} %get-tuple-element.48.k_ref, bf16[1024,128]{1,0:T(8,128)(2,1)S(1)} %get-tuple-element.49.v_ref), custom_call_target="tpu_custom_call" | custom-call | flops 536870912 | bytes 2097152 | tf_op jit(solution)/shard_map/local/pallas_call | solution.py:230
  127.4 3.4 %local.3.local_ref = f32[512,512]{1,0:T(8,128)S(1)} custom-call(bf16[1024,512]{1,0:T(8,128)(2,1)S(1)} %copy-done.1, bf16[1024,128]{1,0:T(8,128)(2,1)S(1)} %get-tuple-element.48.k_ref, bf16[1024,128]{1,0:T(8,128)(2,1)S(1)} %get-tuple-element.49.v_ref), custom_call_target="tpu_custom_call" | custom-call | flops 536870912 | bytes 2097152 | tf_op jit(solution)/shard_map/local/pallas_call | solution.py:230
  130.9 1.7 mix.2.refs_0_
  133.4 1.6 mix.3.refs_1_
  135.1 2.3 %collective-permute-start.19 = (bf16[512,512]{1,0:T(8,128)(2,1)S(1)}, bf16[512,512]{1,0:T(8,128)(2,1)S(1)}, u32[]{:S(2)}, u32[]{:S(2)}) collective-permute-start(bf16[512,512]{1,0:T(8,128)(2,1)S(1)} %mix.3.refs_1_), channel_id=1, source_target_pairs={{0,6},{1,7},{2,0},{3,1},{4,2},{5,3},{6,4},{7,5},{8,14},{9,15},{10,... | collective-permute-start | bytes 1572872 | tf_op jit(solution)/shard_map/ppermute | solution.py:43
  137.9 2.1 %collective-permute-start.26 = (bf16[512,512]{1,0:T(8,128)(2,1)S(1)}, bf16[512,512]{1,0:T(8,128)(2,1)}, u32[]{:S(2)}, u32[]{:S(2)}) collective-permute-start(bf16[512,512]{1,0:T(8,128)(2,1)S(1)} %mix.2.refs_0_), channel_id=1, source_target_pairs={{0,6},{1,7},{2,0},{3,1},{4,2},{5,3},{6,4},{7,5},{8,14},{9,15},{10,... | collective-permute-start | bytes 1572872 | tf_op jit(solution)/shard_map/ppermute | solution.py:43
  140.0 4.6 %collective-permute-start.21 = (bf16[512,512]{1,0:T(8,128)(2,1)S(1)}, bf16[512,512]{1,0:T(8,128)(2,1)S(1)}, u32[]{:S(2)}, u32[]{:S(2)}) collective-permute-start(bf16[512,512]{1,0:T(8,128)(2,1)S(1)} %mix.2.refs_0_), channel_id=1, source_target_pairs={{0,1},{1,0},{2,3},{3,2},{4,5},{5,4},{6,7},{7,6},{8,9},{9,8},{10,11... | collective-permute-start | bytes 1572872 | tf_op jit(solution)/shard_map/ppermute | solution.py:49
  144.6 7.9 %collective-permute-start.22 = (bf16[512,512]{1,0:T(8,128)(2,1)S(1)}, bf16[512,512]{1,0:T(8,128)(2,1)S(1)}, u32[]{:S(2)}, u32[]{:S(2)}) collective-permute-start(bf16[512,512]{1,0:T(8,128)(2,1)S(1)} %mix.3.refs_1_), channel_id=1, source_target_pairs={{0,1},{1,0},{2,3},{3,2},{4,5},{5,4},{6,7},{7,6},{8,9},{9,8},{10,11... | collective-permute-start | bytes 1572872 | tf_op jit(solution)/shard_map/ppermute | solution.py:49
  152.5 1.6 collective-permute-start.24
  154.1 1.2 collective-permute-done.23.refs_5_
  155.4 4.4 %collective-permute-start.25 = (bf16[512,512]{1,0:T(8,128)(2,1)}, bf16[512,512]{1,0:T(8,128)(2,1)}, u32[]{:S(2)}, u32[]{:S(2)}) collective-permute-start(bf16[512,512]{1,0:T(8,128)(2,1)} %collective-permute-done.23.refs_5_), channel_id=1, source_target_pairs={{0,1},{1,0},{2,3},{3,2},{4,5},{5,4},{6,7},{7,6},{8,9},{9,8},{10,11... | collective-permute-start | bytes 1572872 | tf_op jit(solution)/shard_map/ppermute | solution.py:49
  159.8 2.2 %collective-permute-start.27 = (bf16[512,512]{1,0:T(8,128)(2,1)}, bf16[512,512]{1,0:T(8,128)(2,1)}, u32[]{:S(2)}, u32[]{:S(2)}) collective-permute-start(bf16[512,512]{1,0:T(8,128)(2,1)} %collective-permute-done.26.refs_8_), channel_id=1, source_target_pairs={{0,1},{1,0},{2,3},{3,2},{4,5},{5,4},{6,7},{7,6},{8,9},{9,8},{10,11... | collective-permute-start | bytes 1572872 | tf_op jit(solution)/shard_map/ppermute | solution.py:49
  163.6 1.5 collective-permute-start.18
  165.9 1.2 collective-permute-start.20
  167.2 2.2 %copy-done.2 = bf16[32,256,256]{2,1,0:T(8,128)(2,1)S(1)} copy-done((bf16[32,256,256]{2,1,0:T(8,128)(2,1)S(1)}, bf16[32,256,256]{2,1,0:T(8,128)(2,1)}, u32[]{:S(2)}) %copy-start.2) | copy-done | bytes 4194328
  169.4 1.0 copy-done.4
  170.5 1.0 copy-done.6
  171.5 1.0 copy-done.8
  172.6 6.9 %out.1 = (f32[1024,512]{1,0:T(8,128)S(1)}, bf16[2,512,512]{2,1,0:T(8,128)(2,1)S(1)}) custom-call(s32[12]{0:T(128)S(1)} %stack.87.order, bf16[512,512]{1,0:T(8,128)(2,1)S(1)} %mix.2.refs_0_, bf16[512,512]{1,0:T(8,128)(2,1)S(1)} %mix.3.refs_1_, bf16[512,512]{1,0:T(8,128)(2,1)S(1)} %copy-done.4, bf16[512,512]{1,0:T(8,128)(2,1)S(1)} %copy-done.6, ...), custom_call_target="tpu_custom_call" | custom-call | flops 3221225472 | bytes 16777216 | tf_op jit(solution)/shard_map/out/pallas_call | solution.py:310
  179.5 1.1 collective-permute-start.29
  182.9 1.7 add.229
  (92 shorter events, 11.5 us)
Async XLA Ops:
  6.5 103.1 %all-gather.5.cloned.1.call-start = ((), (), s32[]{:S(2)}) async-start(), calls=%async_computation | async-start | bytes 4718592 | tf_op jit(solution)/shard_map/all_gather | solution.py:39
  8.1 12.8 %collective-permute-start.3 = (bf16[128,256]{1,0:T(8,128)(2,1)S(1)}, bf16[128,256]{1,0:T(8,128)(2,1)S(1)}, u32[]{:S(2)}, u32[]{:S(2)}) collective-permute-start(bf16[128,256]{1,0:T(8,128)(2,1)S(1)} %constant_dynamic-update-slice_fusion), channel_id=1, source_target_pairs={{0,8},{8,16},{16,24},{24,32},{32,40},{40,48},{48,56},{56,0},{64,72... | collective-permute-start | bytes 196616 | tf_op jit(solution)/shard_map/ppermute | solution.py:23
  10.6 14.8 %collective-permute-start = (bf16[128,512]{1,0:T(8,128)(2,1)}, bf16[128,512]{1,0:T(8,128)(2,1)S(1)}, u32[]{:S(2)}, u32[]{:S(2)}) collective-permute-start(bf16[128,512]{1,0:T(8,128)(2,1)} %param.11), channel_id=1, source_target_pairs={{0,64},{8,72},{16,80},{24,88},{32,96},{40,104},{48,112},{56,120},{... | collective-permute-start | bytes 393224 | tf_op jit(solution)/shard_map/ppermute | solution.py:33
  11.9 13.5 %collective-permute-start.1 = (bf16[128,512]{1,0:T(8,128)(2,1)}, bf16[128,512]{1,0:T(8,128)(2,1)S(1)}, u32[]{:S(2)}, u32[]{:S(2)}) collective-permute-start(bf16[128,512]{1,0:T(8,128)(2,1)} %param.11), channel_id=1, source_target_pairs={{0,128},{8,136},{16,144},{24,152},{32,160},{40,168},{48,176},{56,1... | collective-permute-start | bytes 393224 | tf_op jit(solution)/shard_map/ppermute | solution.py:33
  14.5 10.8 %collective-permute-start.2 = (bf16[128,512]{1,0:T(8,128)(2,1)}, bf16[128,512]{1,0:T(8,128)(2,1)S(1)}, u32[]{:S(2)}, u32[]{:S(2)}) collective-permute-start(bf16[128,512]{1,0:T(8,128)(2,1)} %param.11), channel_id=1, source_target_pairs={{0,192},{8,200},{16,208},{24,216},{32,224},{40,232},{48,240},{56,2... | collective-permute-start | bytes 393224 | tf_op jit(solution)/shard_map/ppermute | solution.py:33
  15.6 12.6 %collective-permute-start.5 = (bf16[512,128]{1,0:T(8,128)(2,1)}, bf16[512,128]{1,0:T(8,128)(2,1)S(1)}, u32[]{:S(2)}, u32[]{:S(2)}) collective-permute-start(bf16[512,128]{1,0:T(8,128)(2,1)} %param.14), channel_id=1, source_target_pairs={{0,0},{32,1},{64,2},{96,3},{128,4},{160,5},{192,6},{224,7},{1,8},{... | collective-permute-start | bytes 393224 | tf_op jit(solution)/shard_map/ppermute | solution.py:58
  20.8 4.5 %collective-permute-start.4 = (bf16[128,256]{1,0:T(8,128)(2,1)S(1)}, bf16[128,256]{1,0:T(8,128)(2,1)S(1)}, u32[]{:S(2)}, u32[]{:S(2)}) collective-permute-start(bf16[128,256]{1,0:T(8,128)(2,1)S(1)} %constant_dynamic-update-slice_fusion), channel_id=1, source_target_pairs={{0,56},{8,0},{16,8},{24,16},{32,24},{40,32},{48,40},{56,48},{64,12... | collective-permute-start | bytes 196616 | tf_op jit(solution)/shard_map/ppermute | solution.py:23
  28.3 20.4 %collective-permute-start.6 = (bf16[3,128,256]{2,1,0:T(8,128)(2,1)S(1)}, bf16[3,128,256]{2,1,0:T(8,128)(2,1)S(1)}, u32[]{:S(2)}, u32[]{:S(2)}) collective-permute-start(bf16[3,128,256]{2,1,0:T(8,128)(2,1)S(1)} %pad_maximum_fusion.3), channel_id=1, source_target_pairs={{0,24},{8,32},{16,40},{24,48},{32,56},{40,0},{48,8},{56,16},{64,88... | collective-permute-start | bytes 589832 | tf_op jit(solution)/shard_map/ppermute | solution.py:23
  36.6 6.1 %collective-permute-start.7 = (bf16[2,128,256]{2,1,0:T(8,128)(2,1)S(1)}, bf16[2,128,256]{2,1,0:T(8,128)(2,1)S(1)}, u32[]{:S(2)}, u32[]{:S(2)}) collective-permute-start(bf16[2,128,256]{2,1,0:T(8,128)(2,1)S(1)} %pad_maximum_fusion.4), channel_id=1, source_target_pairs={{0,40},{8,48},{16,56},{24,0},{32,8},{40,16},{48,24},{56,32},{64,10... | collective-permute-start | bytes 393224 | tf_op jit(solution)/shard_map/ppermute | solution.py:23
  48.7 118.5 %all-gather.7.cloned.1.call-start = ((), (), s32[]{:S(2)}) async-start(), calls=%async_computation.1 | async-start | bytes 4718592 | tf_op jit(solution)/shard_map/all_gather | solution.py:39
  49.2 30.0 %collective-permute-start.8 = (bf16[10,128,256]{2,1,0:T(8,128)(2,1)S(1)}, bf16[10,128,256]{2,1,0:T(8,128)(2,1)S(1)}, u32[]{:S(2)}, u32[]{:S(2)}) collective-permute-start(bf16[10,128,256]{2,1,0:T(8,128)(2,1)S(1)} %pad_maximum_fusion.refs_4_), channel_id=1, source_target_pairs={{0,64},{8,72},{16,80},{24,88},{32,96},{40,104},{48,112},{56,120},{... | collective-permute-start | bytes 1966088 | tf_op jit(solution)/shard_map/ppermute | solution.py:33
  51.8 27.6 %collective-permute-start.9 = (bf16[10,128,256]{2,1,0:T(8,128)(2,1)S(1)}, bf16[10,128,256]{2,1,0:T(8,128)(2,1)S(1)}, u32[]{:S(2)}, u32[]{:S(2)}) collective-permute-start(bf16[10,128,256]{2,1,0:T(8,128)(2,1)S(1)} %pad_maximum_fusion.refs_4_), channel_id=1, source_target_pairs={{0,128},{8,136},{16,144},{24,152},{32,160},{40,168},{48,176},{56,1... | collective-permute-start | bytes 1966088 | tf_op jit(solution)/shard_map/ppermute | solution.py:33
  51.8 28.9 %collective-permute-start.10 = (bf16[10,128,256]{2,1,0:T(8,128)(2,1)S(1)}, bf16[10,128,256]{2,1,0:T(8,128)(2,1)S(1)}, u32[]{:S(2)}, u32[]{:S(2)}) collective-permute-start(bf16[10,128,256]{2,1,0:T(8,128)(2,1)S(1)} %pad_maximum_fusion.refs_4_), channel_id=1, source_target_pairs={{0,192},{8,200},{16,208},{24,216},{32,224},{40,232},{48,240},{56,2... | collective-permute-start | bytes 1966088 | tf_op jit(solution)/shard_map/ppermute | solution.py:33
  81.7 3.5 %copy-start = (bf16[1024,4096]{1,0:T(8,128)(2,1)S(1)}, bf16[1024,4096]{1,0:T(8,128)(2,1)}, u32[]{:S(2)}) copy-start(bf16[1024,4096]{1,0:T(8,128)(2,1)} %norm.1.refs_0_.refs_1_.refs_2_.refs_3_) | copy-start | bytes 25165828
  85.2 22.4 %copy-start.11 = (f32[4]{0:T(128)S(1)}, f32[4]{0:T(128)}, u32[]{:S(2)}) copy-start(f32[4]{0:T(128)} %param.15) | copy-start | bytes 52
  90.0 5.3 %collective-permute-start.11 = (bf16[136,128]{1,0:T(8,128)(2,1)S(1)}, bf16[136,128]{1,0:T(8,128)(2,1)S(1)}, u32[]{:S(2)}, u32[]{:S(2)}) collective-permute-start(bf16[136,128]{1,0:T(8,128)(2,1)S(1)} %get-tuple-element.61), channel_id=1, source_target_pairs={{0,8},{8,0},{16,24},{24,16},{32,40},{40,32},{48,56},{56,48},{64,72... | collective-permute-start | bytes 104456 | tf_op jit(solution)/shard_map/ppermute | solution.py:29
  95.3 4.9 %collective-permute-start.12 = (bf16[136,128]{1,0:T(8,128)(2,1)S(1)}, bf16[136,128]{1,0:T(8,128)(2,1)S(1)}, u32[]{:S(2)}, u32[]{:S(2)}) collective-permute-start(bf16[136,128]{1,0:T(8,128)(2,1)S(1)} %fusion.6), channel_id=1, source_target_pairs={{0,16},{8,24},{16,0},{24,8},{32,48},{40,56},{48,32},{56,40},{64,80... | collective-permute-start | bytes 104456 | tf_op jit(solution)/shard_map/ppermute | solution.py:29
  100.2 9.3 %collective-permute-start.13 = (bf16[136,128]{1,0:T(8,128)(2,1)S(1)}, bf16[136,128]{1,0:T(8,128)(2,1)S(1)}, u32[]{:S(2)}, u32[]{:S(2)}) collective-permute-start(bf16[136,128]{1,0:T(8,128)(2,1)S(1)} %fusion.7), channel_id=1, source_target_pairs={{0,32},{8,40},{16,48},{24,56},{32,0},{40,8},{48,16},{56,24},{64,96... | collective-permute-start | bytes 104456 | tf_op jit(solution)/shard_map/ppermute | solution.py:29
  109.6 21.2 %collective-permute-start.16 = (bf16[136,128]{1,0:T(8,128)(2,1)S(1)}, bf16[136,128]{1,0:T(8,128)(2,1)S(1)}, u32[]{:S(2)}, u32[]{:S(2)}) collective-permute-start(bf16[136,128]{1,0:T(8,128)(2,1)S(1)} %convert_add_fusion), channel_id=1, source_target_pairs={{0,192},{8,200},{16,208},{24,216},{32,224},{40,232},{48,240},{56,2... | collective-permute-start | bytes 104456 | tf_op jit(solution)/shard_map/ppermute | solution.py:33
  112.1 18.7 %collective-permute-start.15 = (bf16[136,128]{1,0:T(8,128)(2,1)S(1)}, bf16[136,128]{1,0:T(8,128)(2,1)S(1)}, u32[]{:S(2)}, u32[]{:S(2)}) collective-permute-start(bf16[136,128]{1,0:T(8,128)(2,1)S(1)} %convert_add_fusion), channel_id=1, source_target_pairs={{0,128},{8,136},{16,144},{24,152},{32,160},{40,168},{48,176},{56,1... | collective-permute-start | bytes 104456 | tf_op jit(solution)/shard_map/ppermute | solution.py:33
  112.2 18.6 %collective-permute-start.14 = (bf16[136,128]{1,0:T(8,128)(2,1)S(1)}, bf16[136,128]{1,0:T(8,128)(2,1)S(1)}, u32[]{:S(2)}, u32[]{:S(2)}) collective-permute-start(bf16[136,128]{1,0:T(8,128)(2,1)S(1)} %convert_add_fusion), channel_id=1, source_target_pairs={{0,64},{8,72},{16,80},{24,88},{32,96},{40,104},{48,112},{56,120},{... | collective-permute-start | bytes 104456 | tf_op jit(solution)/shard_map/ppermute | solution.py:33
  112.8 18.1 %copy-start.9 = (f32[1,128,128]{2,1,0:T(8,128)S(1)}, f32[1,128,128]{2,1,0:T(8,128)}, u32[]{:S(2)}) copy-start(f32[1,128,128]{2,1,0:T(8,128)} %param.16) | copy-start | bytes 196612
  122.7 8.1 %copy-start.10 = (f32[1,128]{1,0:T(1,128)S(1)}, f32[1,128]{1,0:T(1,128)}, u32[]{:S(2)}) copy-start(f32[1,128]{1,0:T(1,128)} %param.17) | copy-start | bytes 1540
  122.7 1.2 copy-start.1
  132.6 12.0 %collective-permute-start.17 = (bf16[512,512]{1,0:T(8,128)(2,1)S(1)}, bf16[512,512]{1,0:T(8,128)(2,1)S(1)}, u32[]{:S(2)}, u32[]{:S(2)}) collective-permute-start(bf16[512,512]{1,0:T(8,128)(2,1)S(1)} %mix.2.refs_0_), channel_id=1, source_target_pairs={{0,2},{1,3},{2,4},{3,5},{4,6},{5,7},{6,0},{7,1},{8,10},{9,11},{10,... | collective-permute-start | bytes 1572872 | tf_op jit(solution)/shard_map/ppermute | solution.py:43
  135.1 17.4 %collective-permute-start.19 = (bf16[512,512]{1,0:T(8,128)(2,1)S(1)}, bf16[512,512]{1,0:T(8,128)(2,1)S(1)}, u32[]{:S(2)}, u32[]{:S(2)}) collective-permute-start(bf16[512,512]{1,0:T(8,128)(2,1)S(1)} %mix.3.refs_1_), channel_id=1, source_target_pairs={{0,6},{1,7},{2,0},{3,1},{4,2},{5,3},{6,4},{7,5},{8,14},{9,15},{10,... | collective-permute-start | bytes 1572872 | tf_op jit(solution)/shard_map/ppermute | solution.py:43
  137.3 18.0 %collective-permute-start.23 = (bf16[512,512]{1,0:T(8,128)(2,1)S(1)}, bf16[512,512]{1,0:T(8,128)(2,1)}, u32[]{:S(2)}, u32[]{:S(2)}) collective-permute-start(bf16[512,512]{1,0:T(8,128)(2,1)S(1)} %mix.3.refs_1_), channel_id=1, source_target_pairs={{0,2},{1,3},{2,4},{3,5},{4,6},{5,7},{6,0},{7,1},{8,10},{9,11},{10,... | collective-permute-start | bytes 1572872 | tf_op jit(solution)/shard_map/ppermute | solution.py:43
  137.9 21.9 %collective-permute-start.26 = (bf16[512,512]{1,0:T(8,128)(2,1)S(1)}, bf16[512,512]{1,0:T(8,128)(2,1)}, u32[]{:S(2)}, u32[]{:S(2)}) collective-permute-start(bf16[512,512]{1,0:T(8,128)(2,1)S(1)} %mix.2.refs_0_), channel_id=1, source_target_pairs={{0,6},{1,7},{2,0},{3,1},{4,2},{5,3},{6,4},{7,5},{8,14},{9,15},{10,... | collective-permute-start | bytes 1572872 | tf_op jit(solution)/shard_map/ppermute | solution.py:43
  140.0 22.0 %collective-permute-start.21 = (bf16[512,512]{1,0:T(8,128)(2,1)S(1)}, bf16[512,512]{1,0:T(8,128)(2,1)S(1)}, u32[]{:S(2)}, u32[]{:S(2)}) collective-permute-start(bf16[512,512]{1,0:T(8,128)(2,1)S(1)} %mix.2.refs_0_), channel_id=1, source_target_pairs={{0,1},{1,0},{2,3},{3,2},{4,5},{5,4},{6,7},{7,6},{8,9},{9,8},{10,11... | collective-permute-start | bytes 1572872 | tf_op jit(solution)/shard_map/ppermute | solution.py:49
  144.6 18.2 %collective-permute-start.22 = (bf16[512,512]{1,0:T(8,128)(2,1)S(1)}, bf16[512,512]{1,0:T(8,128)(2,1)S(1)}, u32[]{:S(2)}, u32[]{:S(2)}) collective-permute-start(bf16[512,512]{1,0:T(8,128)(2,1)S(1)} %mix.3.refs_1_), channel_id=1, source_target_pairs={{0,1},{1,0},{2,3},{3,2},{4,5},{5,4},{6,7},{7,6},{8,9},{9,8},{10,11... | collective-permute-start | bytes 1572872 | tf_op jit(solution)/shard_map/ppermute | solution.py:49
  152.5 12.6 %collective-permute-start.24 = (bf16[512,512]{1,0:T(8,128)(2,1)S(1)}, bf16[512,512]{1,0:T(8,128)(2,1)S(1)}, u32[]{:S(2)}, u32[]{:S(2)}) collective-permute-start(bf16[512,512]{1,0:T(8,128)(2,1)S(1)} %collective-permute-done.17.refs_4_), channel_id=1, source_target_pairs={{0,1},{1,0},{2,3},{3,2},{4,5},{5,4},{6,7},{7,6},{8,9},{9,8},{10,11... | collective-permute-start | bytes 1572872 | tf_op jit(solution)/shard_map/ppermute | solution.py:49
  155.4 11.8 %collective-permute-start.25 = (bf16[512,512]{1,0:T(8,128)(2,1)}, bf16[512,512]{1,0:T(8,128)(2,1)}, u32[]{:S(2)}, u32[]{:S(2)}) collective-permute-start(bf16[512,512]{1,0:T(8,128)(2,1)} %collective-permute-done.23.refs_5_), channel_id=1, source_target_pairs={{0,1},{1,0},{2,3},{3,2},{4,5},{5,4},{6,7},{7,6},{8,9},{9,8},{10,11... | collective-permute-start | bytes 1572872 | tf_op jit(solution)/shard_map/ppermute | solution.py:49
  159.8 7.4 %collective-permute-start.27 = (bf16[512,512]{1,0:T(8,128)(2,1)}, bf16[512,512]{1,0:T(8,128)(2,1)}, u32[]{:S(2)}, u32[]{:S(2)}) collective-permute-start(bf16[512,512]{1,0:T(8,128)(2,1)} %collective-permute-done.26.refs_8_), channel_id=1, source_target_pairs={{0,1},{1,0},{2,3},{3,2},{4,5},{5,4},{6,7},{7,6},{8,9},{9,8},{10,11... | collective-permute-start | bytes 1572872 | tf_op jit(solution)/shard_map/ppermute | solution.py:49
  162.0 0.8 copy-start.3
  162.8 4.4 %collective-permute-start.28 = (bf16[512,512]{1,0:T(8,128)(2,1)S(1)}, bf16[512,512]{1,0:T(8,128)(2,1)}, u32[]{:S(2)}, u32[]{:S(2)}) collective-permute-start(bf16[512,512]{1,0:T(8,128)(2,1)S(1)} %collective-permute-done.19.refs_9_), channel_id=1, source_target_pairs={{0,1},{1,0},{2,3},{3,2},{4,5},{5,4},{6,7},{7,6},{8,9},{9,8},{10,11... | collective-permute-start | bytes 1572872 | tf_op jit(solution)/shard_map/ppermute | solution.py:49
  162.8 0.8 copy-start.5
  163.6 15.9 %collective-permute-start.18 = (bf16[512,512]{1,0:T(8,128)(2,1)S(1)}, bf16[512,512]{1,0:T(8,128)(2,1)S(1)}, u32[]{:S(2)}, u32[]{:S(2)}) collective-permute-start(bf16[512,512]{1,0:T(8,128)(2,1)S(1)} %collective-permute-done.17.refs_4_), channel_id=1, source_target_pairs={{0,2},{1,3},{2,4},{3,5},{4,6},{5,7},{6,0},{7,1},{8,10},{9,11},{10,... | collective-permute-start | bytes 1572872 | tf_op jit(solution)/shard_map/ppermute | solution.py:43
  165.1 0.8 copy-start.7
  165.9 13.6 %collective-permute-start.20 = (bf16[512,512]{1,0:T(8,128)(2,1)S(1)}, bf16[512,512]{1,0:T(8,128)(2,1)S(1)}, u32[]{:S(2)}, u32[]{:S(2)}) collective-permute-start(bf16[512,512]{1,0:T(8,128)(2,1)S(1)} %collective-permute-done.19.refs_9_), channel_id=1, source_target_pairs={{0,6},{1,7},{2,0},{3,1},{4,2},{5,3},{6,4},{7,5},{8,14},{9,15},{10,... | collective-permute-start | bytes 1572872 | tf_op jit(solution)/shard_map/ppermute | solution.py:43
  167.2 2.2 %copy-start.2 = (bf16[32,256,256]{2,1,0:T(8,128)(2,1)S(1)}, bf16[32,256,256]{2,1,0:T(8,128)(2,1)}, u32[]{:S(2)}) copy-start(bf16[32,256,256]{2,1,0:T(8,128)(2,1)} %all-gather.7.cloned.1.call-done) | copy-start | bytes 12582916
  169.4 1.0 copy-start.4
  170.5 1.0 copy-start.6
  171.5 1.0 copy-start.8
  179.5 2.7 %collective-permute-start.29 = (bf16[512,512]{1,0:T(8,128)(2,1)S(1)}, bf16[512,512]{1,0:T(8,128)(2,1)S(1)}, u32[]{:S(2)}, u32[]{:S(2)}) collective-permute-start(bf16[512,512]{1,0:T(8,128)(2,1)S(1)} %collective-permute-done.18.mixed_0), channel_id=1, source_target_pairs={{0,1},{1,0},{2,3},{3,2},{4,5},{5,4},{6,7},{7,6},{8,9},{9,8},{10,11... | collective-permute-start | bytes 1572872 | tf_op jit(solution)/shard_map/ppermute | solution.py:49
  180.6 2.3 %collective-permute-start.30 = (bf16[512,512]{1,0:T(8,128)(2,1)S(1)}, bf16[512,512]{1,0:T(8,128)(2,1)S(1)}, u32[]{:S(2)}, u32[]{:S(2)}) collective-permute-start(bf16[512,512]{1,0:T(8,128)(2,1)S(1)} %collective-permute-done.20.mixed_1), channel_id=1, source_target_pairs={{0,1},{1,0},{2,3},{3,2},{4,5},{5,4},{6,7},{7,6},{8,9},{9,8},{10,11... | collective-permute-start | bytes 1572872 | tf_op jit(solution)/shard_map/ppermute | solution.py:49
Sparse Core Ops, SparseCore 0:
  48.8 57.2 all-gather.4
  108.0 56.0 all-gather.6
where the time goes:
time: 192 us; the launch traced here: 191 us
  starting transfers between devices  72.3 us (38%)
  Pallas kernels  45.7 us (24%)
  waiting for transfers between devices  41.9 us (22%)
  local copies, waits for them, and re-layouts  14.2 us (7%)
  between operations  13.9 us (7%)
  other arithmetic  3.48 us (2%)
    ppermute x8, starting transfers between devices, core_swap(): return lax.ppermute(block, 'head', [(h, h ^ 1) for h in range(HEADS)])  22 us
    ppermute x9, waiting for transfers between devices, y_move(): lax.ppermute(block, 'seq', [(y * NZ + z, (y + distance) % NY * NZ + z) fo...  14.4 us
    ppermute x4, waiting for transfers between devices, z_move(): lax.ppermute(block, 'seq', [(y * NZ + z, y * NZ + (z + distance) % NZ) fo...  14 us
    unnamed x39, local copies, waits for them, and re-layouts  13.3 us
    ppermute x9, starting transfers between devices, y_move(): lax.ppermute(block, 'seq', [(y * NZ + z, (y + distance) % NY * NZ + z) fo...  13.2 us
    ppermute x4, starting transfers between devices, z_move(): lax.ppermute(block, 'seq', [(y * NZ + z, y * NZ + (z + distance) % NZ) fo...  11.7 us
    ppermute x3, starting transfers between devices, z_swap(): return lax.ppermute(block, 'seq', [(s, s ^ bit) for s in range(SEQ)])  11.7 us
    pallas_call x1, Pallas kernels, norm_call(): pl.pallas_call(norm_kernel, out_shape=jax.ShapeDtypeStruct((rows, width),...  11.4 us
  transfers between devices with their start and end apart: 33, of which 13 were waited for; matrix products, arithmetic and copies ran while one was open for 2% of the time, Pallas kernels for 23%

commit v1 on v0

--- a/solution.py
+++ b/solution.py
@@ -153,7 +153,7 @@
 def kv_kernel(*refs):
     x_refs, pieces = refs[:COLUMNS], refs[COLUMNS : COLUMNS + NY]
     k_ref, v_ref, delta_ref, held, sems = refs[COLUMNS + NY :]
-    copies = fetch([piece.at[pl.ds(0, NZ)] for piece in pieces], [held.at[:, e] for e in range(NY)], sems)
+    copies = fetch(pieces, [held.at[:, e] for e in range(NY)], sems)
     for copy in copies:
         arrived(copy)
     each = NZ // COLUMNS
@@ -280,12 +280,9 @@
         target = weights.at[p] if p < count else rest_ref.at[p - count]
         mine = [
             pltpu.make_async_copy(
-                w_hbm.at[order[p], order[count + 2 + j], :, n * HD : (n + 1) * HD],
-                target.at[n * 2 * HD : (n + 1) * 2 * HD, j * HD : (j + 1) * HD],
-                sems.at[p, 2 * j + n],
+                w_hbm.at[order[p], order[count + 2 + j]], target.at[:, j * HD : (j + 1) * HD], sems.at[p, j]
             )
             for j in range(NY)
-            for n in range(2)
         ]
         for copy in mine:
             copy.start()
@@ -321,7 +318,7 @@
         out_specs=[vmem, vmem],
         scratch_shapes=[
             pltpu.VMEM((count, 4 * HD, 4 * HD), BF16),
-            pltpu.SemaphoreType.DMA((count + 2, 2 * NY)),
+            pltpu.SemaphoreType.DMA((count + 2, NY)),
         ],
         cost_estimate=pl.CostEstimate(flops=4 * count * SEG * 16 * HD * HD, bytes_accessed=(2 * count + 4) << 20, transcendentals=0),
         compiler_params=pltpu.CompilerParams(vmem_limit_bytes=VMEM_LIMIT),
@@ -361,8 +358,7 @@
     wkv = jnp.concatenate([wk, wv], axis=1)
     wq_1, wq_2, wq_3 = y_move(wq, 1), y_move(wq, 2), y_move(wq, -1)
     one, back = z_move(wkv, 1), z_move(wkv, -1)
-    wo_own = spread_wo(wo)
-    wq_1, wq_2, wq_3, one, back, wo_own = together((wq_1, wq_2, wq_3, one, back, wo_own))
+    wq_1, wq_2, wq_3, one, back = together((wq_1, wq_2, wq_3, one, back))
     wq_y = jnp.stack([wq, wq_1, wq_2, wq_3])
     trio = jnp.stack([back, wkv, one])
     wkv_p, wkv_m = z_move(trio, 3), z_move(trio[1:], -3)
@@ -372,14 +368,15 @@
         [wkv[None], back[None], wkv_m[1:], wkv_m[:1], wkv_p[2:], wkv_p[1:2], wkv_p[:1], one[None]]
     )
     wkv_z = lax.dynamic_slice_in_dim(jnp.concatenate([wkv_z, wkv_z[:-1]]), (NZ - z) % NZ, NZ)
-    half = wo_own.shape[0] // 2
-    wo_own = jnp.concatenate([wo_own[:half], wo_own[half:]], axis=1).reshape(2, HD, 2 * HD)
-    packed = jnp.concatenate([wkv_z, wo_own])
-    packs = [packed, y_move(packed, 1), y_move(packed, 2), y_move(packed, -1)]
+    wkv_z, wo = together((wkv_z, wo))
+    packs = [wkv_z, y_move(wkv_z, 1), y_move(wkv_z, 2), y_move(wkv_z, -1)]
+    wo_own = spread_wo(wo)
     normed = norm_call(tokens, norm_gain, order)
-    *packs, normed = together((*packs, normed))
+    *packs, normed, wo_own = together((*packs, normed, wo_own))
+    wo_y = [wo_own, y_move(wo_own, 1), y_move(wo_own, 2), y_move(wo_own, -1)]
     keys, values, delta = kv_call(normed, packs)
-    wo_y = jnp.stack([pack[NZ:].reshape(half, 2 * HD) for pack in packs])
+    delta, *wo_y = together((delta, *wo_y))
+    wo_y = jnp.stack(wo_y)
     wo_gathered = z_gather(wo_y)
 
     total = delta[0] + delta[1]

time: 192 us -> 182 us (0.948)
  waiting for transfers between devices: 41.9 us -> 29.7 us
    ppermute x9 -> x12, waiting for transfers between devices: 14.4 us -> 5.47 us  [y_move(): lax.ppermute(block, 'seq', [(y * NZ + z, (y + distance) % NY * NZ + z) fo...]
    ppermute x9 -> x12, starting transfers between devices: 13.2 us -> 20.3 us  [y_move(): lax.ppermute(block, 'seq', [(y * NZ + z, (y + distance) % NY * NZ + z) fo...]
    ppermute x8, starting transfers between devices: 22 us -> 15.7 us  [core_swap(): return lax.ppermute(block, 'head', [(h, h ^ 1) for h in range(HEADS)])]
    ppermute x4, waiting for transfers between devices: 14 us -> 8.42 us  [z_move(): lax.ppermute(block, 'seq', [(y * NZ + z, y * NZ + (z + distance) % NZ) fo...]
    ppermute x6, waiting for transfers between devices: 1.25 us -> 5.94 us  [x_move(): lax.ppermute(block, 'head', [(2 * x + c, 2 * ((x + distance) % NX) + c) f...]
    ppermute x1, starting transfers between devices: 5.22 us -> 8.11 us  [spread_wo(): return lax.ppermute(block, ('seq', 'head'), pairs)]
    ppermute x1, waiting for transfers between devices: 2.87 us -> 0.01 us  [spread_wo(): return lax.ppermute(block, ('seq', 'head'), pairs)]
    unnamed x39 -> x41, local copies, waits for them, and re-layouts: 13.3 us -> 13.2 us
  transfers between devices with their start and end apart: 33 -> 36, of which waited for: 13 -> 13; matrix products, arithmetic and copies ran while one was open for 2% -> 3% of each run, Pallas kernels for 23% -> 24%
where the time goes in v1:
time: 182 us; the launch traced here: 181 us
  starting transfers between devices  74.1 us (41%)
  Pallas kernels  45.4 us (25%)
  waiting for transfers between devices  29.7 us (16%)
  local copies, waits for them, and re-layouts  14.1 us (8%)
  between operations  13.9 us (8%)
  other arithmetic  3.35 us (2%)
    ppermute x12, starting transfers between devices, y_move(): lax.ppermute(block, 'seq', [(y * NZ + z, (y + distance) % NY * NZ + z) fo...  20.3 us
    ppermute x8, starting transfers between devices, core_swap(): return lax.ppermute(block, 'head', [(h, h ^ 1) for h in range(HEADS)])  15.7 us
    unnamed x41, local copies, waits for them, and re-layouts  13.2 us
    pallas_call x1, Pallas kernels, norm_call(): pl.pallas_call(norm_kernel, out_shape=jax.ShapeDtypeStruct((rows, width),...  11.5 us
    ppermute x3, starting transfers between devices, z_swap(): return lax.ppermute(block, 'seq', [(s, s ^ bit) for s in range(SEQ)])  10.4 us
    ppermute x4, starting transfers between devices, z_move(): lax.ppermute(block, 'seq', [(y * NZ + z, y * NZ + (z + distance) % NZ) fo...  10.4 us
    pallas_call x1, Pallas kernels, q_call(): pl.pallas_call(q_kernel, grid=(rows // tile,), out_shape=jax.ShapeDtypeSt...  9.93 us
    ppermute x6, starting transfers between devices, x_move(): lax.ppermute(block, 'head', [(2 * x + c, 2 * ((x + distance) % NX) + c) f...  9.24 us
  transfers between devices with their start and end apart: 36, of which 13 were waited for; matrix products, arithmetic and copies ran while one was open for 3% of the time, Pallas kernels for 24%

profile of v1, /device:TPU:1, one launch (start us, length us, event | category | flops | bytes accessed | tf_op | source)
XLA Modules:
  0.0 180.6 jit_solution(1097439855204985485)
XLA Ops:
  6.5 2.1 %collective-permute-start = (bf16[128,512]{1,0:T(8,128)(2,1)}, bf16[128,512]{1,0:T(8,128)(2,1)S(1)}, u32[]{:S(2)}, u32[]{:S(2)}) collective-permute-start(bf16[128,512]{1,0:T(8,128)(2,1)} %param.11), channel_id=1, source_target_pairs={{0,64},{8,72},{16,80},{24,88},{32,96},{40,104},{48,112},{56,120},{... | collective-permute-start | bytes 393224 | tf_op jit(solution)/shard_map/ppermute | solution.py:33
  8.7 2.6 %collective-permute-start.1 = (bf16[128,512]{1,0:T(8,128)(2,1)}, bf16[128,512]{1,0:T(8,128)(2,1)S(1)}, u32[]{:S(2)}, u32[]{:S(2)}) collective-permute-start(bf16[128,512]{1,0:T(8,128)(2,1)} %param.11), channel_id=1, source_target_pairs={{0,128},{8,136},{16,144},{24,152},{32,160},{40,168},{48,176},{56,1... | collective-permute-start | bytes 393224 | tf_op jit(solution)/shard_map/ppermute | solution.py:33
  11.3 1.1 collective-permute-start.2
  13.9 1.7 collective-permute-start.3
  15.6 4.0 %collective-permute-start.4 = (bf16[128,256]{1,0:T(8,128)(2,1)S(1)}, bf16[128,256]{1,0:T(8,128)(2,1)S(1)}, u32[]{:S(2)}, u32[]{:S(2)}) collective-permute-start(bf16[128,256]{1,0:T(8,128)(2,1)S(1)} %constant_dynamic-update-slice_fusion), channel_id=1, source_target_pairs={{0,56},{8,0},{16,8},{24,16},{32,24},{40,32},{48,40},{56,48},{64,12... | collective-permute-start | bytes 196616 | tf_op jit(solution)/shard_map/ppermute | solution.py:23
  19.6 1.6 collective-permute-done.3
  21.2 4.4 %collective-permute-start.5 = (bf16[3,128,256]{2,1,0:T(8,128)(2,1)S(1)}, bf16[3,128,256]{2,1,0:T(8,128)(2,1)S(1)}, u32[]{:S(2)}, u32[]{:S(2)}) collective-permute-start(bf16[3,128,256]{2,1,0:T(8,128)(2,1)S(1)} %pad_maximum_fusion.2), channel_id=1, source_target_pairs={{0,24},{8,32},{16,40},{24,48},{32,56},{40,0},{48,8},{56,16},{64,88... | collective-permute-start | bytes 589832 | tf_op jit(solution)/shard_map/ppermute | solution.py:23
  25.9 1.8 pad_maximum_fusion
  27.7 4.9 %collective-permute-done.6 = bf16[2,128,256]{2,1,0:T(8,128)(2,1)S(1)} collective-permute-done((bf16[2,128,256]{2,1,0:T(8,128)(2,1)S(1)}, bf16[2,128,256]{2,1,0:T(8,128)(2,1)S(1)}, u32[]{:S(2)}, u32[]{:S(2)}) %collective-permute-start.6) | collective-permute-done | bytes 131104 | tf_op jit(solution)/shard_map/ppermute | solution.py:23
  32.5 2.0 %collective-permute-done.5 = bf16[3,128,256]{2,1,0:T(8,128)(2,1)S(1)} collective-permute-done((bf16[3,128,256]{2,1,0:T(8,128)(2,1)S(1)}, bf16[3,128,256]{2,1,0:T(8,128)(2,1)S(1)}, u32[]{:S(2)}, u32[]{:S(2)}) %collective-permute-start.5) | collective-permute-done | bytes 196640 | tf_op jit(solution)/shard_map/ppermute | solution.py:23
  35.4 2.5 %collective-permute-start.9 = (bf16[8,128,256]{2,1,0:T(8,128)(2,1)S(1)}, bf16[8,128,256]{2,1,0:T(8,128)(2,1)S(1)}, u32[]{:S(2)}, u32[]{:S(2)}) collective-permute-start(bf16[8,128,256]{2,1,0:T(8,128)(2,1)S(1)} %constant_dynamic-slice_fusion.refs_4_), channel_id=1, source_target_pairs={{0,192},{8,200},{16,208},{24,216},{32,224},{40,232},{48,240},{56,2... | collective-permute-start | bytes 1572872 | tf_op jit(solution)/shard_map/ppermute | solution.py:33
  37.9 8.1 %collective-permute-start.10 = (bf16[512,128]{1,0:T(8,128)(2,1)S(1)}, bf16[512,128]{1,0:T(8,128)(2,1)S(1)}, u32[]{:S(2)}, u32[]{:S(2)}) collective-permute-start(bf16[512,128]{1,0:T(8,128)(2,1)S(1)} %copy-done.11), channel_id=1, source_target_pairs={{0,0},{32,1},{64,2},{96,3},{128,4},{160,5},{192,6},{224,7},{1,8},{... | collective-permute-start | bytes 393224 | tf_op jit(solution)/shard_map/ppermute | solution.py:58
  46.6 11.5 %norm.1.refs_0_.refs_1_.refs_2_.refs_3_ = bf16[1024,4096]{1,0:T(8,128)(2,1)} custom-call(s32[32]{0:T(128)} %fusion.8.order, bf16[1024,4096]{1,0:T(8,128)(2,1)} %x_ref.1, f32[1,4096]{1,0:T(1,128)} %bitcast.56), custom_call_target="tpu_custom_call" | custom-call | flops 25165824 | bytes 16777216 | tf_op jit(solution)/shard_map/norm/pallas_call | solution.py:82
  58.1 1.2 collective-permute-done.7.refs_5_
  59.3 4.2 %collective-permute-done.9.refs_7_ = bf16[8,128,256]{2,1,0:T(8,128)(2,1)S(1)} collective-permute-done((bf16[8,128,256]{2,1,0:T(8,128)(2,1)S(1)}, bf16[8,128,256]{2,1,0:T(8,128)(2,1)S(1)}, u32[]{:S(2)}, u32[]{:S(2)}) %collective-permute-start.9) | collective-permute-done | bytes 524320 | tf_op jit(solution)/shard_map/ppermute | solution.py:33
  63.6 4.7 %collective-permute-start.12 = (bf16[512,128]{1,0:T(8,128)(2,1)S(1)}, bf16[512,128]{1,0:T(8,128)(2,1)S(1)}, u32[]{:S(2)}, u32[]{:S(2)}) collective-permute-start(bf16[512,128]{1,0:T(8,128)(2,1)S(1)} %collective-permute-done.10), channel_id=1, source_target_pairs={{0,128},{8,136},{16,144},{24,152},{32,160},{40,168},{48,176},{56,1... | collective-permute-start | bytes 393224 | tf_op jit(solution)/shard_map/ppermute | solution.py:33
  68.3 3.4 %copy-done = bf16[1024,4096]{1,0:T(8,128)(2,1)S(1)} copy-done((bf16[1024,4096]{1,0:T(8,128)(2,1)S(1)}, bf16[1024,4096]{1,0:T(8,128)(2,1)}, u32[]{:S(2)}) %copy-start) | copy-done | bytes 8388632
  71.7 4.9 %kv.1 = (bf16[1024,128]{1,0:T(8,128)(2,1)S(1)}, bf16[1024,128]{1,0:T(8,128)(2,1)S(1)}, f32[2,136,128]{2,1,0:T(8,128)S(1)}) custom-call(bf16[1024,4096]{1,0:T(8,128)(2,1)S(1)} %copy-done, bf16[1024,4096]{1,0:T(8,128)(2,1)S(1)} %copy-done, bf16[1024,4096]{1,0:T(8,128)(2,1)S(1)} %copy-done, bf16[1024,4096]{1,0:T(8,128)(2,1)S(1)} %copy-done, ...), custom_call_target="tpu_custom_call" | custom-call | flops 2147483648 | bytes 10485760 | tf_op jit(solution)/shard_map/kv/pallas_call | solution.py:191
  77.5 1.6 collective-permute-start.14
  79.1 2.4 %collective-permute-done.14 = bf16[136,128]{1,0:T(8,128)(2,1)S(1)} collective-permute-done((bf16[136,128]{1,0:T(8,128)(2,1)S(1)}, bf16[136,128]{1,0:T(8,128)(2,1)S(1)}, u32[]{:S(2)}, u32[]{:S(2)}) %collective-permute-start.14) | collective-permute-done | bytes 34848 | tf_op jit(solution)/shard_map/ppermute | solution.py:29
  81.5 3.9 %collective-permute-start.15 = (bf16[136,128]{1,0:T(8,128)(2,1)S(1)}, bf16[136,128]{1,0:T(8,128)(2,1)S(1)}, u32[]{:S(2)}, u32[]{:S(2)}) collective-permute-start(bf16[136,128]{1,0:T(8,128)(2,1)S(1)} %fusion.6), channel_id=1, source_target_pairs={{0,16},{8,24},{16,0},{24,8},{32,48},{40,56},{48,32},{56,40},{64,80... | collective-permute-start | bytes 104456 | tf_op jit(solution)/shard_map/ppermute | solution.py:29
  85.4 2.7 %collective-permute-done.15 = bf16[136,128]{1,0:T(8,128)(2,1)S(1)} collective-permute-done((bf16[136,128]{1,0:T(8,128)(2,1)S(1)}, bf16[136,128]{1,0:T(8,128)(2,1)S(1)}, u32[]{:S(2)}, u32[]{:S(2)}) %collective-permute-start.15) | collective-permute-done | bytes 34848 | tf_op jit(solution)/shard_map/ppermute | solution.py:29
  88.1 4.9 %collective-permute-start.16 = (bf16[136,128]{1,0:T(8,128)(2,1)S(1)}, bf16[136,128]{1,0:T(8,128)(2,1)S(1)}, u32[]{:S(2)}, u32[]{:S(2)}) collective-permute-start(bf16[136,128]{1,0:T(8,128)(2,1)S(1)} %fusion.7), channel_id=1, source_target_pairs={{0,32},{8,40},{16,48},{24,56},{32,0},{40,8},{48,16},{56,24},{64,96... | collective-permute-start | bytes 104456 | tf_op jit(solution)/shard_map/ppermute | solution.py:29
  93.1 2.7 %collective-permute-done.16 = bf16[136,128]{1,0:T(8,128)(2,1)S(1)} collective-permute-done((bf16[136,128]{1,0:T(8,128)(2,1)S(1)}, bf16[136,128]{1,0:T(8,128)(2,1)S(1)}, u32[]{:S(2)}, u32[]{:S(2)}) %collective-permute-start.16) | collective-permute-done | bytes 34848 | tf_op jit(solution)/shard_map/ppermute | solution.py:29
  96.4 4.4 %collective-permute-start.19 = (bf16[136,128]{1,0:T(8,128)(2,1)S(1)}, bf16[136,128]{1,0:T(8,128)(2,1)S(1)}, u32[]{:S(2)}, u32[]{:S(2)}) collective-permute-start(bf16[136,128]{1,0:T(8,128)(2,1)S(1)} %convert_add_fusion), channel_id=1, source_target_pairs={{0,192},{8,200},{16,208},{24,216},{32,224},{40,232},{48,240},{56,2... | collective-permute-start | bytes 104456 | tf_op jit(solution)/shard_map/ppermute | solution.py:33
  100.8 1.5 collective-permute-start.18
  103.1 9.9 %q.1.q_ref = bf16[1024,512]{1,0:T(8,128)(2,1)} custom-call(bf16[1024,4096]{1,0:T(8,128)(2,1)} %norm.1.refs_0_.refs_1_.refs_2_.refs_3_, bf16[1024,4096]{1,0:T(8,128)(2,1)} %norm.1.refs_0_.refs_1_.refs_2_.refs_3_, bf16[1024,4096]{1,0:T(8,128)(2,1)} %norm.1.refs_0_.refs_1_.refs_2_.refs_3_, bf16[1024,4096]{1,0:T(8,128)(2,1)} %norm.1.refs_0_.refs_1_.refs_2_.refs_3_, ...), custom_call_target="tpu_custom_call" | custom-call | flops 4294967296 | bytes 12582912 | tf_op jit(solution)/shard_map/q/pallas_call | solution.py:140
  113.1 1.2 copy-done.1
  114.3 3.4 %local.2.local_ref = f32[512,512]{1,0:T(8,128)S(1)} custom-call(bf16[1024,512]{1,0:T(8,128)(2,1)S(1)} %copy-done.1, bf16[1024,128]{1,0:T(8,128)(2,1)S(1)} %get-tuple-element.58.k_ref, bf16[1024,128]{1,0:T(8,128)(2,1)S(1)} %get-tuple-element.59.v_ref), custom_call_target="tpu_custom_call" | custom-call | flops 536870912 | bytes 2097152 | tf_op jit(solution)/shard_map/local/pallas_call | solution.py:230
  117.7 3.4 %local.3.local_ref = f32[512,512]{1,0:T(8,128)S(1)} custom-call(bf16[1024,512]{1,0:T(8,128)(2,1)S(1)} %copy-done.1, bf16[1024,128]{1,0:T(8,128)(2,1)S(1)} %get-tuple-element.58.k_ref, bf16[1024,128]{1,0:T(8,128)(2,1)S(1)} %get-tuple-element.59.v_ref), custom_call_target="tpu_custom_call" | custom-call | flops 536870912 | bytes 2097152 | tf_op jit(solution)/shard_map/local/pallas_call | solution.py:230
  121.3 1.7 mix.2.refs_0_
  123.0 1.7 mix.3.refs_1_
  124.7 3.0 %collective-permute-start.22 = (bf16[512,512]{1,0:T(8,128)(2,1)S(1)}, bf16[512,512]{1,0:T(8,128)(2,1)S(1)}, u32[]{:S(2)}, u32[]{:S(2)}) collective-permute-start(bf16[512,512]{1,0:T(8,128)(2,1)S(1)} %mix.3.refs_1_), channel_id=1, source_target_pairs={{0,6},{1,7},{2,0},{3,1},{4,2},{5,3},{6,4},{7,5},{8,14},{9,15},{10,... | collective-permute-start | bytes 1572872 | tf_op jit(solution)/shard_map/ppermute | solution.py:43
  127.6 2.7 %collective-permute-start.29 = (bf16[512,512]{1,0:T(8,128)(2,1)S(1)}, bf16[512,512]{1,0:T(8,128)(2,1)}, u32[]{:S(2)}, u32[]{:S(2)}) collective-permute-start(bf16[512,512]{1,0:T(8,128)(2,1)S(1)} %mix.2.refs_0_), channel_id=1, source_target_pairs={{0,6},{1,7},{2,0},{3,1},{4,2},{5,3},{6,4},{7,5},{8,14},{9,15},{10,... | collective-permute-start | bytes 1572872 | tf_op jit(solution)/shard_map/ppermute | solution.py:43
  130.3 3.0 %collective-permute-start.24 = (bf16[512,512]{1,0:T(8,128)(2,1)S(1)}, bf16[512,512]{1,0:T(8,128)(2,1)S(1)}, u32[]{:S(2)}, u32[]{:S(2)}) collective-permute-start(bf16[512,512]{1,0:T(8,128)(2,1)S(1)} %mix.2.refs_0_), channel_id=1, source_target_pairs={{0,1},{1,0},{2,3},{3,2},{4,5},{5,4},{6,7},{7,6},{8,9},{9,8},{10,11... | collective-permute-start | bytes 1572872 | tf_op jit(solution)/shard_map/ppermute | solution.py:49
  133.3 2.6 %collective-permute-done.20.refs_4_ = bf16[512,512]{1,0:T(8,128)(2,1)S(1)} collective-permute-done((bf16[512,512]{1,0:T(8,128)(2,1)S(1)}, bf16[512,512]{1,0:T(8,128)(2,1)S(1)}, u32[]{:S(2)}, u32[]{:S(2)}) %collective-permute-start.20) | collective-permute-done | bytes 524320 | tf_op jit(solution)/shard_map/ppermute | solution.py:43
  135.9 5.0 %collective-permute-start.25 = (bf16[512,512]{1,0:T(8,128)(2,1)S(1)}, bf16[512,512]{1,0:T(8,128)(2,1)S(1)}, u32[]{:S(2)}, u32[]{:S(2)}) collective-permute-start(bf16[512,512]{1,0:T(8,128)(2,1)S(1)} %mix.3.refs_1_), channel_id=1, source_target_pairs={{0,1},{1,0},{2,3},{3,2},{4,5},{5,4},{6,7},{7,6},{8,9},{9,8},{10,11... | collective-permute-start | bytes 1572872 | tf_op jit(solution)/shard_map/ppermute | solution.py:49
  140.9 3.0 %collective-permute-start.27 = (bf16[512,512]{1,0:T(8,128)(2,1)S(1)}, bf16[512,512]{1,0:T(8,128)(2,1)S(1)}, u32[]{:S(2)}, u32[]{:S(2)}) collective-permute-start(bf16[512,512]{1,0:T(8,128)(2,1)S(1)} %collective-permute-done.20.refs_4_), channel_id=1, source_target_pairs={{0,1},{1,0},{2,3},{3,2},{4,5},{5,4},{6,7},{7,6},{8,9},{9,8},{10,11... | collective-permute-start | bytes 1572872 | tf_op jit(solution)/shard_map/ppermute | solution.py:49
  143.9 3.3 %collective-permute-done.26.refs_5_ = bf16[512,512]{1,0:T(8,128)(2,1)} collective-permute-done((bf16[512,512]{1,0:T(8,128)(2,1)S(1)}, bf16[512,512]{1,0:T(8,128)(2,1)}, u32[]{:S(2)}, u32[]{:S(2)}) %collective-permute-start.26) | collective-permute-done | bytes 524320 | tf_op jit(solution)/shard_map/ppermute | solution.py:43
  147.1 2.7 %collective-permute-start.28 = (bf16[512,512]{1,0:T(8,128)(2,1)}, bf16[512,512]{1,0:T(8,128)(2,1)}, u32[]{:S(2)}, u32[]{:S(2)}) collective-permute-start(bf16[512,512]{1,0:T(8,128)(2,1)} %collective-permute-done.26.refs_5_), channel_id=1, source_target_pairs={{0,1},{1,0},{2,3},{3,2},{4,5},{5,4},{6,7},{7,6},{8,9},{9,8},{10,11... | collective-permute-start | bytes 1572872 | tf_op jit(solution)/shard_map/ppermute | solution.py:49
  149.9 1.1 collective-permute-start.30
  153.4 3.5 %collective-permute-start.23 = (bf16[512,512]{1,0:T(8,128)(2,1)S(1)}, bf16[512,512]{1,0:T(8,128)(2,1)S(1)}, u32[]{:S(2)}, u32[]{:S(2)}) collective-permute-start(bf16[512,512]{1,0:T(8,128)(2,1)S(1)} %collective-permute-done.22.refs_9_), channel_id=1, source_target_pairs={{0,6},{1,7},{2,0},{3,1},{4,2},{5,3},{6,4},{7,5},{8,14},{9,15},{10,... | collective-permute-start | bytes 1572872 | tf_op jit(solution)/shard_map/ppermute | solution.py:43
  157.1 2.2 %copy-done.2 = bf16[32,512,128]{2,1,0:T(8,128)(2,1)S(1)} copy-done((bf16[32,512,128]{2,1,0:T(8,128)(2,1)S(1)}, bf16[32,512,128]{2,1,0:T(8,128)(2,1)}, u32[]{:S(2)}) %copy-start.2) | copy-done | bytes 4194328
  159.3 1.0 copy-done.4
  160.3 1.0 copy-done.6
  161.3 1.0 copy-done.8
  162.4 6.5 %out.1 = (f32[1024,512]{1,0:T(8,128)S(1)}, bf16[2,512,512]{2,1,0:T(8,128)(2,1)S(1)}) custom-call(s32[12]{0:T(128)S(1)} %stack.99.order, bf16[512,512]{1,0:T(8,128)(2,1)S(1)} %mix.2.refs_0_, bf16[512,512]{1,0:T(8,128)(2,1)S(1)} %mix.3.refs_1_, bf16[512,512]{1,0:T(8,128)(2,1)S(1)} %copy-done.4, bf16[512,512]{1,0:T(8,128)(2,1)S(1)} %copy-done.6, ...), custom_call_target="tpu_custom_call" | custom-call | flops 3221225472 | bytes 16777216 | tf_op jit(solution)/shard_map/out/pallas_call | solution.py:307
  172.1 1.7 add.229
  (93 shorter events, 11.4 us)
Async XLA Ops:
  6.5 31.4 %copy-start.11 = (bf16[512,128]{1,0:T(8,128)(2,1)S(1)}, bf16[512,128]{1,0:T(8,128)(2,1)}, u32[]{:S(2)}) copy-start(bf16[512,128]{1,0:T(8,128)(2,1)} %param.14) | copy-start | bytes 393220
  6.5 89.8 %all-gather.5.cloned.1.call-start = ((), (), s32[]{:S(2)}) async-start(), calls=%async_computation | async-start | bytes 4718592 | tf_op jit(solution)/shard_map/all_gather | solution.py:39
  6.5 14.7 %collective-permute-start = (bf16[128,512]{1,0:T(8,128)(2,1)}, bf16[128,512]{1,0:T(8,128)(2,1)S(1)}, u32[]{:S(2)}, u32[]{:S(2)}) collective-permute-start(bf16[128,512]{1,0:T(8,128)(2,1)} %param.11), channel_id=1, source_target_pairs={{0,64},{8,72},{16,80},{24,88},{32,96},{40,104},{48,112},{56,120},{... | collective-permute-start | bytes 393224 | tf_op jit(solution)/shard_map/ppermute | solution.py:33
  8.7 12.5 %collective-permute-start.1 = (bf16[128,512]{1,0:T(8,128)(2,1)}, bf16[128,512]{1,0:T(8,128)(2,1)S(1)}, u32[]{:S(2)}, u32[]{:S(2)}) collective-permute-start(bf16[128,512]{1,0:T(8,128)(2,1)} %param.11), channel_id=1, source_target_pairs={{0,128},{8,136},{16,144},{24,152},{32,160},{40,168},{48,176},{56,1... | collective-permute-start | bytes 393224 | tf_op jit(solution)/shard_map/ppermute | solution.py:33
  11.3 9.9 %collective-permute-start.2 = (bf16[128,512]{1,0:T(8,128)(2,1)}, bf16[128,512]{1,0:T(8,128)(2,1)S(1)}, u32[]{:S(2)}, u32[]{:S(2)}) collective-permute-start(bf16[128,512]{1,0:T(8,128)(2,1)} %param.11), channel_id=1, source_target_pairs={{0,192},{8,200},{16,208},{24,216},{32,224},{40,232},{48,240},{56,2... | collective-permute-start | bytes 393224 | tf_op jit(solution)/shard_map/ppermute | solution.py:33
  13.9 7.3 %collective-permute-start.3 = (bf16[128,256]{1,0:T(8,128)(2,1)S(1)}, bf16[128,256]{1,0:T(8,128)(2,1)S(1)}, u32[]{:S(2)}, u32[]{:S(2)}) collective-permute-start(bf16[128,256]{1,0:T(8,128)(2,1)S(1)} %constant_dynamic-update-slice_fusion), channel_id=1, source_target_pairs={{0,8},{8,16},{16,24},{24,32},{32,40},{40,48},{48,56},{56,0},{64,72... | collective-permute-start | bytes 196616 | tf_op jit(solution)/shard_map/ppermute | solution.py:23
  15.6 5.6 %collective-permute-start.4 = (bf16[128,256]{1,0:T(8,128)(2,1)S(1)}, bf16[128,256]{1,0:T(8,128)(2,1)S(1)}, u32[]{:S(2)}, u32[]{:S(2)}) collective-permute-start(bf16[128,256]{1,0:T(8,128)(2,1)S(1)} %constant_dynamic-update-slice_fusion), channel_id=1, source_target_pairs={{0,56},{8,0},{16,8},{24,16},{32,24},{40,32},{48,40},{56,48},{64,12... | collective-permute-start | bytes 196616 | tf_op jit(solution)/shard_map/ppermute | solution.py:23
  21.2 13.3 %collective-permute-start.5 = (bf16[3,128,256]{2,1,0:T(8,128)(2,1)S(1)}, bf16[3,128,256]{2,1,0:T(8,128)(2,1)S(1)}, u32[]{:S(2)}, u32[]{:S(2)}) collective-permute-start(bf16[3,128,256]{2,1,0:T(8,128)(2,1)S(1)} %pad_maximum_fusion.2), channel_id=1, source_target_pairs={{0,24},{8,32},{16,40},{24,48},{32,56},{40,0},{48,8},{56,16},{64,88... | collective-permute-start | bytes 589832 | tf_op jit(solution)/shard_map/ppermute | solution.py:23
  25.6 6.9 %collective-permute-start.6 = (bf16[2,128,256]{2,1,0:T(8,128)(2,1)S(1)}, bf16[2,128,256]{2,1,0:T(8,128)(2,1)S(1)}, u32[]{:S(2)}, u32[]{:S(2)}) collective-permute-start(bf16[2,128,256]{2,1,0:T(8,128)(2,1)S(1)} %pad_maximum_fusion.3), channel_id=1, source_target_pairs={{0,40},{8,48},{16,56},{24,0},{32,8},{40,16},{48,24},{56,32},{64,10... | collective-permute-start | bytes 393224 | tf_op jit(solution)/shard_map/ppermute | solution.py:23
  34.5 122.5 %all-gather.7.cloned.1.call-start = ((), (), s32[]{:S(2)}) async-start(), calls=%async_computation.1 | async-start | bytes 4718592 | tf_op jit(solution)/shard_map/all_gather | solution.py:39
  34.9 24.4 %collective-permute-start.7 = (bf16[8,128,256]{2,1,0:T(8,128)(2,1)S(1)}, bf16[8,128,256]{2,1,0:T(8,128)(2,1)S(1)}, u32[]{:S(2)}, u32[]{:S(2)}) collective-permute-start(bf16[8,128,256]{2,1,0:T(8,128)(2,1)S(1)} %constant_dynamic-slice_fusion.refs_4_), channel_id=1, source_target_pairs={{0,64},{8,72},{16,80},{24,88},{32,96},{40,104},{48,112},{56,120},{... | collective-permute-start | bytes 1572872 | tf_op jit(solution)/shard_map/ppermute | solution.py:33
  35.4 23.9 %collective-permute-start.8 = (bf16[8,128,256]{2,1,0:T(8,128)(2,1)S(1)}, bf16[8,128,256]{2,1,0:T(8,128)(2,1)S(1)}, u32[]{:S(2)}, u32[]{:S(2)}) collective-permute-start(bf16[8,128,256]{2,1,0:T(8,128)(2,1)S(1)} %constant_dynamic-slice_fusion.refs_4_), channel_id=1, source_target_pairs={{0,128},{8,136},{16,144},{24,152},{32,160},{40,168},{48,176},{56,1... | collective-permute-start | bytes 1572872 | tf_op jit(solution)/shard_map/ppermute | solution.py:33
  35.4 28.1 %collective-permute-start.9 = (bf16[8,128,256]{2,1,0:T(8,128)(2,1)S(1)}, bf16[8,128,256]{2,1,0:T(8,128)(2,1)S(1)}, u32[]{:S(2)}, u32[]{:S(2)}) collective-permute-start(bf16[8,128,256]{2,1,0:T(8,128)(2,1)S(1)} %constant_dynamic-slice_fusion.refs_4_), channel_id=1, source_target_pairs={{0,192},{8,200},{16,208},{24,216},{32,224},{40,232},{48,240},{56,2... | collective-permute-start | bytes 1572872 | tf_op jit(solution)/shard_map/ppermute | solution.py:33
  37.9 20.2 %collective-permute-start.10 = (bf16[512,128]{1,0:T(8,128)(2,1)S(1)}, bf16[512,128]{1,0:T(8,128)(2,1)S(1)}, u32[]{:S(2)}, u32[]{:S(2)}) collective-permute-start(bf16[512,128]{1,0:T(8,128)(2,1)S(1)} %copy-done.11), channel_id=1, source_target_pairs={{0,0},{32,1},{64,2},{96,3},{128,4},{160,5},{192,6},{224,7},{1,8},{... | collective-permute-start | bytes 393224 | tf_op jit(solution)/shard_map/ppermute | solution.py:58
  46.6 46.5 %copy-start.12 = (f32[4]{0:T(128)S(1)}, f32[4]{0:T(128)}, u32[]{:S(2)}) copy-start(f32[4]{0:T(128)} %param.15) | copy-start | bytes 52
  63.6 13.0 %collective-permute-start.11 = (bf16[512,128]{1,0:T(8,128)(2,1)S(1)}, bf16[512,128]{1,0:T(8,128)(2,1)S(1)}, u32[]{:S(2)}, u32[]{:S(2)}) collective-permute-start(bf16[512,128]{1,0:T(8,128)(2,1)S(1)} %collective-permute-done.10), channel_id=1, source_target_pairs={{0,64},{8,72},{16,80},{24,88},{32,96},{40,104},{48,112},{56,120},{... | collective-permute-start | bytes 393224 | tf_op jit(solution)/shard_map/ppermute | solution.py:33
  63.6 13.0 %collective-permute-start.12 = (bf16[512,128]{1,0:T(8,128)(2,1)S(1)}, bf16[512,128]{1,0:T(8,128)(2,1)S(1)}, u32[]{:S(2)}, u32[]{:S(2)}) collective-permute-start(bf16[512,128]{1,0:T(8,128)(2,1)S(1)} %collective-permute-done.10), channel_id=1, source_target_pairs={{0,128},{8,136},{16,144},{24,152},{32,160},{40,168},{48,176},{56,1... | collective-permute-start | bytes 393224 | tf_op jit(solution)/shard_map/ppermute | solution.py:33
  68.3 8.3 %collective-permute-start.13 = (bf16[512,128]{1,0:T(8,128)(2,1)S(1)}, bf16[512,128]{1,0:T(8,128)(2,1)S(1)}, u32[]{:S(2)}, u32[]{:S(2)}) collective-permute-start(bf16[512,128]{1,0:T(8,128)(2,1)S(1)} %collective-permute-done.10), channel_id=1, source_target_pairs={{0,192},{8,200},{16,208},{24,216},{32,224},{40,232},{48,240},{56,2... | collective-permute-start | bytes 393224 | tf_op jit(solution)/shard_map/ppermute | solution.py:33
  68.3 3.4 %copy-start = (bf16[1024,4096]{1,0:T(8,128)(2,1)S(1)}, bf16[1024,4096]{1,0:T(8,128)(2,1)}, u32[]{:S(2)}) copy-start(bf16[1024,4096]{1,0:T(8,128)(2,1)} %norm.1.refs_0_.refs_1_.refs_2_.refs_3_) | copy-start | bytes 25165828
  77.5 4.0 %collective-permute-start.14 = (bf16[136,128]{1,0:T(8,128)(2,1)S(1)}, bf16[136,128]{1,0:T(8,128)(2,1)S(1)}, u32[]{:S(2)}, u32[]{:S(2)}) collective-permute-start(bf16[136,128]{1,0:T(8,128)(2,1)S(1)} %get-tuple-element.75), channel_id=1, source_target_pairs={{0,8},{8,0},{16,24},{24,16},{32,40},{40,32},{48,56},{56,48},{64,72... | collective-permute-start | bytes 104456 | tf_op jit(solution)/shard_map/ppermute | solution.py:29
  81.5 6.6 %collective-permute-start.15 = (bf16[136,128]{1,0:T(8,128)(2,1)S(1)}, bf16[136,128]{1,0:T(8,128)(2,1)S(1)}, u32[]{:S(2)}, u32[]{:S(2)}) collective-permute-start(bf16[136,128]{1,0:T(8,128)(2,1)S(1)} %fusion.6), channel_id=1, source_target_pairs={{0,16},{8,24},{16,0},{24,8},{32,48},{40,56},{48,32},{56,40},{64,80... | collective-permute-start | bytes 104456 | tf_op jit(solution)/shard_map/ppermute | solution.py:29
  88.1 7.6 %collective-permute-start.16 = (bf16[136,128]{1,0:T(8,128)(2,1)S(1)}, bf16[136,128]{1,0:T(8,128)(2,1)S(1)}, u32[]{:S(2)}, u32[]{:S(2)}) collective-permute-start(bf16[136,128]{1,0:T(8,128)(2,1)S(1)} %fusion.7), channel_id=1, source_target_pairs={{0,32},{8,40},{16,48},{24,56},{32,0},{40,8},{48,16},{56,24},{64,96... | collective-permute-start | bytes 104456 | tf_op jit(solution)/shard_map/ppermute | solution.py:29
  96.4 24.8 %collective-permute-start.19 = (bf16[136,128]{1,0:T(8,128)(2,1)S(1)}, bf16[136,128]{1,0:T(8,128)(2,1)S(1)}, u32[]{:S(2)}, u32[]{:S(2)}) collective-permute-start(bf16[136,128]{1,0:T(8,128)(2,1)S(1)} %convert_add_fusion), channel_id=1, source_target_pairs={{0,192},{8,200},{16,208},{24,216},{32,224},{40,232},{48,240},{56,2... | collective-permute-start | bytes 104456 | tf_op jit(solution)/shard_map/ppermute | solution.py:33
  100.8 20.4 %collective-permute-start.18 = (bf16[136,128]{1,0:T(8,128)(2,1)S(1)}, bf16[136,128]{1,0:T(8,128)(2,1)S(1)}, u32[]{:S(2)}, u32[]{:S(2)}) collective-permute-start(bf16[136,128]{1,0:T(8,128)(2,1)S(1)} %convert_add_fusion), channel_id=1, source_target_pairs={{0,128},{8,136},{16,144},{24,152},{32,160},{40,168},{48,176},{56,1... | collective-permute-start | bytes 104456 | tf_op jit(solution)/shard_map/ppermute | solution.py:33
  102.2 18.9 %collective-permute-start.17 = (bf16[136,128]{1,0:T(8,128)(2,1)S(1)}, bf16[136,128]{1,0:T(8,128)(2,1)S(1)}, u32[]{:S(2)}, u32[]{:S(2)}) collective-permute-start(bf16[136,128]{1,0:T(8,128)(2,1)S(1)} %convert_add_fusion), channel_id=1, source_target_pairs={{0,64},{8,72},{16,80},{24,88},{32,96},{40,104},{48,112},{56,120},{... | collective-permute-start | bytes 104456 | tf_op jit(solution)/shard_map/ppermute | solution.py:33
  103.1 18.1 %copy-start.9 = (f32[1,128,128]{2,1,0:T(8,128)S(1)}, f32[1,128,128]{2,1,0:T(8,128)}, u32[]{:S(2)}) copy-start(f32[1,128,128]{2,1,0:T(8,128)} %param.16) | copy-start | bytes 196612
  113.0 8.1 %copy-start.10 = (f32[1,128]{1,0:T(1,128)S(1)}, f32[1,128]{1,0:T(1,128)}, u32[]{:S(2)}) copy-start(f32[1,128]{1,0:T(1,128)} %param.17) | copy-start | bytes 1540
  113.0 1.2 copy-start.1
  122.9 13.0 %collective-permute-start.20 = (bf16[512,512]{1,0:T(8,128)(2,1)S(1)}, bf16[512,512]{1,0:T(8,128)(2,1)S(1)}, u32[]{:S(2)}, u32[]{:S(2)}) collective-permute-start(bf16[512,512]{1,0:T(8,128)(2,1)S(1)} %mix.2.refs_0_), channel_id=1, source_target_pairs={{0,2},{1,3},{2,4},{3,5},{4,6},{5,7},{6,0},{7,1},{8,10},{9,11},{10,... | collective-permute-start | bytes 1572872 | tf_op jit(solution)/shard_map/ppermute | solution.py:43
  124.7 16.2 %collective-permute-start.22 = (bf16[512,512]{1,0:T(8,128)(2,1)S(1)}, bf16[512,512]{1,0:T(8,128)(2,1)S(1)}, u32[]{:S(2)}, u32[]{:S(2)}) collective-permute-start(bf16[512,512]{1,0:T(8,128)(2,1)S(1)} %mix.3.refs_1_), channel_id=1, source_target_pairs={{0,6},{1,7},{2,0},{3,1},{4,2},{5,3},{6,4},{7,5},{8,14},{9,15},{10,... | collective-permute-start | bytes 1572872 | tf_op jit(solution)/shard_map/ppermute | solution.py:43
  127.6 19.5 %collective-permute-start.26 = (bf16[512,512]{1,0:T(8,128)(2,1)S(1)}, bf16[512,512]{1,0:T(8,128)(2,1)}, u32[]{:S(2)}, u32[]{:S(2)}) collective-permute-start(bf16[512,512]{1,0:T(8,128)(2,1)S(1)} %mix.3.refs_1_), channel_id=1, source_target_pairs={{0,2},{1,3},{2,4},{3,5},{4,6},{5,7},{6,0},{7,1},{8,10},{9,11},{10,... | collective-permute-start | bytes 1572872 | tf_op jit(solution)/shard_map/ppermute | solution.py:43
  127.6 22.3 %collective-permute-start.29 = (bf16[512,512]{1,0:T(8,128)(2,1)S(1)}, bf16[512,512]{1,0:T(8,128)(2,1)}, u32[]{:S(2)}, u32[]{:S(2)}) collective-permute-start(bf16[512,512]{1,0:T(8,128)(2,1)S(1)} %mix.2.refs_0_), channel_id=1, source_target_pairs={{0,6},{1,7},{2,0},{3,1},{4,2},{5,3},{6,4},{7,5},{8,14},{9,15},{10,... | collective-permute-start | bytes 1572872 | tf_op jit(solution)/shard_map/ppermute | solution.py:43
  130.3 20.7 %collective-permute-start.24 = (bf16[512,512]{1,0:T(8,128)(2,1)S(1)}, bf16[512,512]{1,0:T(8,128)(2,1)S(1)}, u32[]{:S(2)}, u32[]{:S(2)}) collective-permute-start(bf16[512,512]{1,0:T(8,128)(2,1)S(1)} %mix.2.refs_0_), channel_id=1, source_target_pairs={{0,1},{1,0},{2,3},{3,2},{4,5},{5,4},{6,7},{7,6},{8,9},{9,8},{10,11... | collective-permute-start | bytes 1572872 | tf_op jit(solution)/shard_map/ppermute | solution.py:49
  135.9 15.9 %collective-permute-start.25 = (bf16[512,512]{1,0:T(8,128)(2,1)S(1)}, bf16[512,512]{1,0:T(8,128)(2,1)S(1)}, u32[]{:S(2)}, u32[]{:S(2)}) collective-permute-start(bf16[512,512]{1,0:T(8,128)(2,1)S(1)} %mix.3.refs_1_), channel_id=1, source_target_pairs={{0,1},{1,0},{2,3},{3,2},{4,5},{5,4},{6,7},{7,6},{8,9},{9,8},{10,11... | collective-permute-start | bytes 1572872 | tf_op jit(solution)/shard_map/ppermute | solution.py:49
  140.9 11.7 %collective-permute-start.27 = (bf16[512,512]{1,0:T(8,128)(2,1)S(1)}, bf16[512,512]{1,0:T(8,128)(2,1)S(1)}, u32[]{:S(2)}, u32[]{:S(2)}) collective-permute-start(bf16[512,512]{1,0:T(8,128)(2,1)S(1)} %collective-permute-done.20.refs_4_), channel_id=1, source_target_pairs={{0,1},{1,0},{2,3},{3,2},{4,5},{5,4},{6,7},{7,6},{8,9},{9,8},{10,11... | collective-permute-start | bytes 1572872 | tf_op jit(solution)/shard_map/ppermute | solution.py:49
  147.1 9.9 %collective-permute-start.28 = (bf16[512,512]{1,0:T(8,128)(2,1)}, bf16[512,512]{1,0:T(8,128)(2,1)}, u32[]{:S(2)}, u32[]{:S(2)}) collective-permute-start(bf16[512,512]{1,0:T(8,128)(2,1)} %collective-permute-done.26.refs_5_), channel_id=1, source_target_pairs={{0,1},{1,0},{2,3},{3,2},{4,5},{5,4},{6,7},{7,6},{8,9},{9,8},{10,11... | collective-permute-start | bytes 1572872 | tf_op jit(solution)/shard_map/ppermute | solution.py:49
  149.9 7.2 %collective-permute-start.30 = (bf16[512,512]{1,0:T(8,128)(2,1)}, bf16[512,512]{1,0:T(8,128)(2,1)}, u32[]{:S(2)}, u32[]{:S(2)}) collective-permute-start(bf16[512,512]{1,0:T(8,128)(2,1)} %collective-permute-done.29.refs_8_), channel_id=1, source_target_pairs={{0,1},{1,0},{2,3},{3,2},{4,5},{5,4},{6,7},{7,6},{8,9},{9,8},{10,11... | collective-permute-start | bytes 1572872 | tf_op jit(solution)/shard_map/ppermute | solution.py:49
  151.0 0.8 copy-start.3
  151.8 5.3 %collective-permute-start.31 = (bf16[512,512]{1,0:T(8,128)(2,1)S(1)}, bf16[512,512]{1,0:T(8,128)(2,1)}, u32[]{:S(2)}, u32[]{:S(2)}) collective-permute-start(bf16[512,512]{1,0:T(8,128)(2,1)S(1)} %collective-permute-done.22.refs_9_), channel_id=1, source_target_pairs={{0,1},{1,0},{2,3},{3,2},{4,5},{5,4},{6,7},{7,6},{8,9},{9,8},{10,11... | collective-permute-start | bytes 1572872 | tf_op jit(solution)/shard_map/ppermute | solution.py:49
  152.6 16.4 %collective-permute-start.21 = (bf16[512,512]{1,0:T(8,128)(2,1)S(1)}, bf16[512,512]{1,0:T(8,128)(2,1)S(1)}, u32[]{:S(2)}, u32[]{:S(2)}) collective-permute-start(bf16[512,512]{1,0:T(8,128)(2,1)S(1)} %collective-permute-done.20.refs_4_), channel_id=1, source_target_pairs={{0,2},{1,3},{2,4},{3,5},{4,6},{5,7},{6,0},{7,1},{8,10},{9,11},{10,... | collective-permute-start | bytes 1572872 | tf_op jit(solution)/shard_map/ppermute | solution.py:43
  152.6 0.8 copy-start.7
  153.4 15.5 %collective-permute-start.23 = (bf16[512,512]{1,0:T(8,128)(2,1)S(1)}, bf16[512,512]{1,0:T(8,128)(2,1)S(1)}, u32[]{:S(2)}, u32[]{:S(2)}) collective-permute-start(bf16[512,512]{1,0:T(8,128)(2,1)S(1)} %collective-permute-done.22.refs_9_), channel_id=1, source_target_pairs={{0,6},{1,7},{2,0},{3,1},{4,2},{5,3},{6,4},{7,5},{8,14},{9,15},{10,... | collective-permute-start | bytes 1572872 | tf_op jit(solution)/shard_map/ppermute | solution.py:43
  157.1 2.2 %copy-start.2 = (bf16[32,512,128]{2,1,0:T(8,128)(2,1)S(1)}, bf16[32,512,128]{2,1,0:T(8,128)(2,1)}, u32[]{:S(2)}) copy-start(bf16[32,512,128]{2,1,0:T(8,128)(2,1)} %all-gather.7.cloned.1.call-done) | copy-start | bytes 12582916
  159.3 1.0 copy-start.4
  160.3 1.0 copy-start.6
  161.3 1.0 copy-start.8
  169.0 2.4 %collective-permute-start.32 = (bf16[512,512]{1,0:T(8,128)(2,1)S(1)}, bf16[512,512]{1,0:T(8,128)(2,1)S(1)}, u32[]{:S(2)}, u32[]{:S(2)}) collective-permute-start(bf16[512,512]{1,0:T(8,128)(2,1)S(1)} %collective-permute-done.21.mixed_0), channel_id=1, source_target_pairs={{0,1},{1,0},{2,3},{3,2},{4,5},{5,4},{6,7},{7,6},{8,9},{9,8},{10,11... | collective-permute-start | bytes 1572872 | tf_op jit(solution)/shard_map/ppermute | solution.py:49
  169.8 2.3 %collective-permute-start.33 = (bf16[512,512]{1,0:T(8,128)(2,1)S(1)}, bf16[512,512]{1,0:T(8,128)(2,1)S(1)}, u32[]{:S(2)}, u32[]{:S(2)}) collective-permute-start(bf16[512,512]{1,0:T(8,128)(2,1)S(1)} %collective-permute-done.23.mixed_1), channel_id=1, source_target_pairs={{0,1},{1,0},{2,3},{3,2},{4,5},{5,4},{6,7},{7,6},{8,9},{9,8},{10,11... | collective-permute-start | bytes 1572872 | tf_op jit(solution)/shard_map/ppermute | solution.py:49
  (1 other events, 0.8 us)
Sparse Core Ops, SparseCore 0:
  34.7 61.6 all-gather.4
  98.1 56.0 all-gather.6

commit v2 on v1

--- a/solution.py
+++ b/solution.py
@@ -274,7 +274,7 @@
 
 
 def out_kernel(count, order, *refs):
-    mixed_refs, (w_hbm, out_ref, rest_ref, weights, sems) = refs[: 2 * count], refs[2 * count :]
+    mixed_refs, (w_hbm, out_ref, rest_ref, weights, mixed, sems, mixed_sems) = refs[: 2 * count], refs[2 * count :]
     copies = []
     for p in range(count + 2):
         target = weights.at[p] if p < count else rest_ref.at[p - count]
@@ -284,6 +284,10 @@
             )
             for j in range(NY)
         ]
+        if p < count:
+            mine += [
+                pltpu.make_async_copy(mixed_refs[n], mixed.at[n], mixed_sems.at[n]) for n in (2 * p, 2 * p + 1)
+            ]
         for copy in mine:
             copy.start()
         copies.append(mine)
@@ -292,7 +296,7 @@
         for copy in copies[p]:
             copy.wait()
         for s in range(2):
-            term = jnp.dot(mixed_refs[2 * p + s][...], weights[p], preferred_element_type=F32)
+            term = jnp.dot(mixed[2 * p + s], weights[p], preferred_element_type=F32)
             totals[s] = term if totals[s] is None else totals[s] + term
     for s in range(2):
         out_ref[s * SEG : (s + 1) * SEG, :] = totals[s]
@@ -312,16 +316,18 @@
         ],
         in_specs=[
             pl.BlockSpec(memory_space=pltpu.SMEM),
-            *[vmem] * (2 * count),
+            *[pl.BlockSpec(memory_space=pl.ANY)] * (2 * count),
             pl.BlockSpec(memory_space=pltpu.HBM),
         ],
         out_specs=[vmem, vmem],
         scratch_shapes=[
             pltpu.VMEM((count, 4 * HD, 4 * HD), BF16),
+            pltpu.VMEM((2 * count, SEG, 4 * HD), BF16),
             pltpu.SemaphoreType.DMA((count + 2, NY)),
+            pltpu.SemaphoreType.DMA((2 * count,)),
         ],
         cost_estimate=pl.CostEstimate(flops=4 * count * SEG * 16 * HD * HD, bytes_accessed=(2 * count + 4) << 20, transcendentals=0),
-        compiler_params=pltpu.CompilerParams(vmem_limit_bytes=VMEM_LIMIT),
+        compiler_params=pltpu.CompilerParams(vmem_limit_bytes=57 << 20),
         name="out",
     )(order, *[part for piece in pieces for part in piece], weight)
 

time: 182 us -> 182 us (level)
  local copies, waits for them, and re-layouts: 14.1 us -> 10.7 us
  Pallas kernels: 45.4 us -> 47.8 us
    unnamed x41 -> x43, local copies, waits for them, and re-layouts: 13.2 us -> 9.22 us
    pallas_call x1, Pallas kernels: 6.55 us -> 8.91 us  [out_call(): pl.pallas_call(functools.partial(out_kernel, count), out_shape=[jax.Shape...]
  transfers between devices with their start and end apart: 36 -> 36, of which waited for: 13 -> 12; matrix products, arithmetic and copies ran while one was open for 3% -> 3% of each run, Pallas kernels for 24% -> 26%
where the time goes in v2:
time: 182 us; the launch traced here: 180 us
  starting transfers between devices  74.3 us (41%)
  Pallas kernels  47.8 us (26%)
  waiting for transfers between devices  29.7 us (16%)
  between operations  13.9 us (8%)
  local copies, waits for them, and re-layouts  10.7 us (6%)
  other arithmetic  3.34 us (2%)
    ppermute x12, starting transfers between devices, y_move(): lax.ppermute(block, 'seq', [(y * NZ + z, (y + distance) % NY * NZ + z) fo...  20.3 us
    ppermute x8, starting transfers between devices, core_swap(): return lax.ppermute(block, 'head', [(h, h ^ 1) for h in range(HEADS)])  15.9 us
    pallas_call x1, Pallas kernels, norm_call(): pl.pallas_call(norm_kernel, out_shape=jax.ShapeDtypeStruct((rows, width),...  11.5 us
    ppermute x3, starting transfers between devices, z_swap(): return lax.ppermute(block, 'seq', [(s, s ^ bit) for s in range(SEQ)])  10.4 us
    ppermute x4, starting transfers between devices, z_move(): lax.ppermute(block, 'seq', [(y * NZ + z, y * NZ + (z + distance) % NZ) fo...  10.4 us
    pallas_call x1, Pallas kernels, q_call(): pl.pallas_call(q_kernel, grid=(rows // tile,), out_shape=jax.ShapeDtypeSt...  9.93 us
    ppermute x6, starting transfers between devices, x_move(): lax.ppermute(block, 'head', [(2 * x + c, 2 * ((x + distance) % NX) + c) f...  9.25 us
    unnamed x43, local copies, waits for them, and re-layouts  9.22 us
  transfers between devices with their start and end apart: 36, of which 12 were waited for; matrix products, arithmetic and copies ran while one was open for 3% of the time, Pallas kernels for 26%

profile of v2, /device:TPU:1, one launch (start us, length us, event | category | flops | bytes accessed | tf_op | source)
XLA Modules:
  0.0 179.7 jit_solution(16163427957031644136)
XLA Ops:
  6.5 2.1 %collective-permute-start = (bf16[128,512]{1,0:T(8,128)(2,1)}, bf16[128,512]{1,0:T(8,128)(2,1)S(1)}, u32[]{:S(2)}, u32[]{:S(2)}) collective-permute-start(bf16[128,512]{1,0:T(8,128)(2,1)} %param.11), channel_id=1, source_target_pairs={{0,64},{8,72},{16,80},{24,88},{32,96},{40,104},{48,112},{56,120},{... | collective-permute-start | bytes 393224 | tf_op jit(solution)/shard_map/ppermute | solution.py:33
  8.7 2.6 %collective-permute-start.1 = (bf16[128,512]{1,0:T(8,128)(2,1)}, bf16[128,512]{1,0:T(8,128)(2,1)S(1)}, u32[]{:S(2)}, u32[]{:S(2)}) collective-permute-start(bf16[128,512]{1,0:T(8,128)(2,1)} %param.11), channel_id=1, source_target_pairs={{0,128},{8,136},{16,144},{24,152},{32,160},{40,168},{48,176},{56,1... | collective-permute-start | bytes 393224 | tf_op jit(solution)/shard_map/ppermute | solution.py:33
  11.3 1.1 collective-permute-start.2
  13.9 1.7 collective-permute-start.3
  15.6 4.0 %collective-permute-start.4 = (bf16[128,256]{1,0:T(8,128)(2,1)S(1)}, bf16[128,256]{1,0:T(8,128)(2,1)S(1)}, u32[]{:S(2)}, u32[]{:S(2)}) collective-permute-start(bf16[128,256]{1,0:T(8,128)(2,1)S(1)} %constant_dynamic-update-slice_fusion), channel_id=1, source_target_pairs={{0,56},{8,0},{16,8},{24,16},{32,24},{40,32},{48,40},{56,48},{64,12... | collective-permute-start | bytes 196616 | tf_op jit(solution)/shard_map/ppermute | solution.py:23
  19.6 1.6 collective-permute-done.3
  21.2 4.4 %collective-permute-start.5 = (bf16[3,128,256]{2,1,0:T(8,128)(2,1)S(1)}, bf16[3,128,256]{2,1,0:T(8,128)(2,1)S(1)}, u32[]{:S(2)}, u32[]{:S(2)}) collective-permute-start(bf16[3,128,256]{2,1,0:T(8,128)(2,1)S(1)} %pad_maximum_fusion.2), channel_id=1, source_target_pairs={{0,24},{8,32},{16,40},{24,48},{32,56},{40,0},{48,8},{56,16},{64,88... | collective-permute-start | bytes 589832 | tf_op jit(solution)/shard_map/ppermute | solution.py:23
  25.9 1.8 pad_maximum_fusion
  27.7 4.9 %collective-permute-done.6 = bf16[2,128,256]{2,1,0:T(8,128)(2,1)S(1)} collective-permute-done((bf16[2,128,256]{2,1,0:T(8,128)(2,1)S(1)}, bf16[2,128,256]{2,1,0:T(8,128)(2,1)S(1)}, u32[]{:S(2)}, u32[]{:S(2)}) %collective-permute-start.6) | collective-permute-done | bytes 131104 | tf_op jit(solution)/shard_map/ppermute | solution.py:23
  32.5 2.0 %collective-permute-done.5 = bf16[3,128,256]{2,1,0:T(8,128)(2,1)S(1)} collective-permute-done((bf16[3,128,256]{2,1,0:T(8,128)(2,1)S(1)}, bf16[3,128,256]{2,1,0:T(8,128)(2,1)S(1)}, u32[]{:S(2)}, u32[]{:S(2)}) %collective-permute-start.5) | collective-permute-done | bytes 196640 | tf_op jit(solution)/shard_map/ppermute | solution.py:23
  35.4 2.5 %collective-permute-start.9 = (bf16[8,128,256]{2,1,0:T(8,128)(2,1)S(1)}, bf16[8,128,256]{2,1,0:T(8,128)(2,1)S(1)}, u32[]{:S(2)}, u32[]{:S(2)}) collective-permute-start(bf16[8,128,256]{2,1,0:T(8,128)(2,1)S(1)} %constant_dynamic-slice_fusion.refs_4_), channel_id=1, source_target_pairs={{0,192},{8,200},{16,208},{24,216},{32,224},{40,232},{48,240},{56,2... | collective-permute-start | bytes 1572872 | tf_op jit(solution)/shard_map/ppermute | solution.py:33
  37.9 8.1 %collective-permute-start.10 = (bf16[512,128]{1,0:T(8,128)(2,1)S(1)}, bf16[512,128]{1,0:T(8,128)(2,1)S(1)}, u32[]{:S(2)}, u32[]{:S(2)}) collective-permute-start(bf16[512,128]{1,0:T(8,128)(2,1)S(1)} %copy-done.12), channel_id=1, source_target_pairs={{0,0},{32,1},{64,2},{96,3},{128,4},{160,5},{192,6},{224,7},{1,8},{... | collective-permute-start | bytes 393224 | tf_op jit(solution)/shard_map/ppermute | solution.py:58
  46.6 11.5 %norm.1.refs_0_.refs_1_.refs_2_.refs_3_ = bf16[1024,4096]{1,0:T(8,128)(2,1)} custom-call(s32[32]{0:T(128)} %fusion.8.order, bf16[1024,4096]{1,0:T(8,128)(2,1)} %x_ref.1, f32[1,4096]{1,0:T(1,128)} %bitcast.55), custom_call_target="tpu_custom_call" | custom-call | flops 25165824 | bytes 16777216 | tf_op jit(solution)/shard_map/norm/pallas_call | solution.py:82
  58.1 1.2 collective-permute-done.7.refs_5_
  59.3 4.2 %collective-permute-done.9.refs_7_ = bf16[8,128,256]{2,1,0:T(8,128)(2,1)S(1)} collective-permute-done((bf16[8,128,256]{2,1,0:T(8,128)(2,1)S(1)}, bf16[8,128,256]{2,1,0:T(8,128)(2,1)S(1)}, u32[]{:S(2)}, u32[]{:S(2)}) %collective-permute-start.9) | collective-permute-done | bytes 524320 | tf_op jit(solution)/shard_map/ppermute | solution.py:33
  63.6 4.7 %collective-permute-start.12 = (bf16[512,128]{1,0:T(8,128)(2,1)S(1)}, bf16[512,128]{1,0:T(8,128)(2,1)S(1)}, u32[]{:S(2)}, u32[]{:S(2)}) collective-permute-start(bf16[512,128]{1,0:T(8,128)(2,1)S(1)} %collective-permute-done.10), channel_id=1, source_target_pairs={{0,128},{8,136},{16,144},{24,152},{32,160},{40,168},{48,176},{56,1... | collective-permute-start | bytes 393224 | tf_op jit(solution)/shard_map/ppermute | solution.py:33
  68.3 3.4 %copy-done = bf16[1024,4096]{1,0:T(8,128)(2,1)S(1)} copy-done((bf16[1024,4096]{1,0:T(8,128)(2,1)S(1)}, bf16[1024,4096]{1,0:T(8,128)(2,1)}, u32[]{:S(2)}) %copy-start) | copy-done | bytes 8388632
  71.7 4.9 %kv.1 = (bf16[1024,128]{1,0:T(8,128)(2,1)S(1)}, bf16[1024,128]{1,0:T(8,128)(2,1)S(1)}, f32[2,136,128]{2,1,0:T(8,128)S(1)}) custom-call(bf16[1024,4096]{1,0:T(8,128)(2,1)S(1)} %copy-done, bf16[1024,4096]{1,0:T(8,128)(2,1)S(1)} %copy-done, bf16[1024,4096]{1,0:T(8,128)(2,1)S(1)} %copy-done, bf16[1024,4096]{1,0:T(8,128)(2,1)S(1)} %copy-done, ...), custom_call_target="tpu_custom_call" | custom-call | flops 2147483648 | bytes 10485760 | tf_op jit(solution)/shard_map/kv/pallas_call | solution.py:191
  77.5 1.6 collective-permute-start.14
  79.1 2.4 %collective-permute-done.14 = bf16[136,128]{1,0:T(8,128)(2,1)S(1)} collective-permute-done((bf16[136,128]{1,0:T(8,128)(2,1)S(1)}, bf16[136,128]{1,0:T(8,128)(2,1)S(1)}, u32[]{:S(2)}, u32[]{:S(2)}) %collective-permute-start.14) | collective-permute-done | bytes 34848 | tf_op jit(solution)/shard_map/ppermute | solution.py:29
  81.5 3.9 %collective-permute-start.15 = (bf16[136,128]{1,0:T(8,128)(2,1)S(1)}, bf16[136,128]{1,0:T(8,128)(2,1)S(1)}, u32[]{:S(2)}, u32[]{:S(2)}) collective-permute-start(bf16[136,128]{1,0:T(8,128)(2,1)S(1)} %fusion.6), channel_id=1, source_target_pairs={{0,16},{8,24},{16,0},{24,8},{32,48},{40,56},{48,32},{56,40},{64,80... | collective-permute-start | bytes 104456 | tf_op jit(solution)/shard_map/ppermute | solution.py:29
  85.4 2.7 %collective-permute-done.15 = bf16[136,128]{1,0:T(8,128)(2,1)S(1)} collective-permute-done((bf16[136,128]{1,0:T(8,128)(2,1)S(1)}, bf16[136,128]{1,0:T(8,128)(2,1)S(1)}, u32[]{:S(2)}, u32[]{:S(2)}) %collective-permute-start.15) | collective-permute-done | bytes 34848 | tf_op jit(solution)/shard_map/ppermute | solution.py:29
  88.1 4.9 %collective-permute-start.16 = (bf16[136,128]{1,0:T(8,128)(2,1)S(1)}, bf16[136,128]{1,0:T(8,128)(2,1)S(1)}, u32[]{:S(2)}, u32[]{:S(2)}) collective-permute-start(bf16[136,128]{1,0:T(8,128)(2,1)S(1)} %fusion.7), channel_id=1, source_target_pairs={{0,32},{8,40},{16,48},{24,56},{32,0},{40,8},{48,16},{56,24},{64,96... | collective-permute-start | bytes 104456 | tf_op jit(solution)/shard_map/ppermute | solution.py:29
  93.1 2.7 %collective-permute-done.16 = bf16[136,128]{1,0:T(8,128)(2,1)S(1)} collective-permute-done((bf16[136,128]{1,0:T(8,128)(2,1)S(1)}, bf16[136,128]{1,0:T(8,128)(2,1)S(1)}, u32[]{:S(2)}, u32[]{:S(2)}) %collective-permute-start.16) | collective-permute-done | bytes 34848 | tf_op jit(solution)/shard_map/ppermute | solution.py:29
  96.4 4.4 %collective-permute-start.19 = (bf16[136,128]{1,0:T(8,128)(2,1)S(1)}, bf16[136,128]{1,0:T(8,128)(2,1)S(1)}, u32[]{:S(2)}, u32[]{:S(2)}) collective-permute-start(bf16[136,128]{1,0:T(8,128)(2,1)S(1)} %convert_add_fusion), channel_id=1, source_target_pairs={{0,192},{8,200},{16,208},{24,216},{32,224},{40,232},{48,240},{56,2... | collective-permute-start | bytes 104456 | tf_op jit(solution)/shard_map/ppermute | solution.py:33
  100.8 1.5 collective-permute-start.18
  103.1 9.9 %q.1.q_ref = bf16[1024,512]{1,0:T(8,128)(2,1)} custom-call(bf16[1024,4096]{1,0:T(8,128)(2,1)} %norm.1.refs_0_.refs_1_.refs_2_.refs_3_, bf16[1024,4096]{1,0:T(8,128)(2,1)} %norm.1.refs_0_.refs_1_.refs_2_.refs_3_, bf16[1024,4096]{1,0:T(8,128)(2,1)} %norm.1.refs_0_.refs_1_.refs_2_.refs_3_, bf16[1024,4096]{1,0:T(8,128)(2,1)} %norm.1.refs_0_.refs_1_.refs_2_.refs_3_, ...), custom_call_target="tpu_custom_call" | custom-call | flops 4294967296 | bytes 12582912 | tf_op jit(solution)/shard_map/q/pallas_call | solution.py:140
  113.1 1.2 copy-done.1
  114.3 3.4 %local.2.local_ref = f32[512,512]{1,0:T(8,128)S(1)} custom-call(bf16[1024,512]{1,0:T(8,128)(2,1)S(1)} %copy-done.1, bf16[1024,128]{1,0:T(8,128)(2,1)S(1)} %get-tuple-element.58.k_ref, bf16[1024,128]{1,0:T(8,128)(2,1)S(1)} %get-tuple-element.59.v_ref), custom_call_target="tpu_custom_call" | custom-call | flops 536870912 | bytes 2097152 | tf_op jit(solution)/shard_map/local/pallas_call | solution.py:230
  117.7 3.4 %local.3.local_ref = f32[512,512]{1,0:T(8,128)S(1)} custom-call(bf16[1024,512]{1,0:T(8,128)(2,1)S(1)} %copy-done.1, bf16[1024,128]{1,0:T(8,128)(2,1)S(1)} %get-tuple-element.58.k_ref, bf16[1024,128]{1,0:T(8,128)(2,1)S(1)} %get-tuple-element.59.v_ref), custom_call_target="tpu_custom_call" | custom-call | flops 536870912 | bytes 2097152 | tf_op jit(solution)/shard_map/local/pallas_call | solution.py:230
  121.3 1.7 mix.2.refs_0_
  123.0 1.7 mix.3.refs_1_
  124.7 3.0 %collective-permute-start.22 = (bf16[512,512]{1,0:T(8,128)(2,1)S(1)}, bf16[512,512]{1,0:T(8,128)(2,1)S(1)}, u32[]{:S(2)}, u32[]{:S(2)}) collective-permute-start(bf16[512,512]{1,0:T(8,128)(2,1)S(1)} %mix.3.refs_1_), channel_id=1, source_target_pairs={{0,6},{1,7},{2,0},{3,1},{4,2},{5,3},{6,4},{7,5},{8,14},{9,15},{10,... | collective-permute-start | bytes 1572872 | tf_op jit(solution)/shard_map/ppermute | solution.py:43
  127.6 2.7 %collective-permute-start.29 = (bf16[512,512]{1,0:T(8,128)(2,1)S(1)}, bf16[512,512]{1,0:T(8,128)(2,1)}, u32[]{:S(2)}, u32[]{:S(2)}) collective-permute-start(bf16[512,512]{1,0:T(8,128)(2,1)S(1)} %mix.2.refs_0_), channel_id=1, source_target_pairs={{0,6},{1,7},{2,0},{3,1},{4,2},{5,3},{6,4},{7,5},{8,14},{9,15},{10,... | collective-permute-start | bytes 1572872 | tf_op jit(solution)/shard_map/ppermute | solution.py:43
  130.3 3.0 %collective-permute-start.24 = (bf16[512,512]{1,0:T(8,128)(2,1)S(1)}, bf16[512,512]{1,0:T(8,128)(2,1)S(1)}, u32[]{:S(2)}, u32[]{:S(2)}) collective-permute-start(bf16[512,512]{1,0:T(8,128)(2,1)S(1)} %mix.2.refs_0_), channel_id=1, source_target_pairs={{0,1},{1,0},{2,3},{3,2},{4,5},{5,4},{6,7},{7,6},{8,9},{9,8},{10,11... | collective-permute-start | bytes 1572872 | tf_op jit(solution)/shard_map/ppermute | solution.py:49
  133.3 2.6 %collective-permute-done.20.refs_4_ = bf16[512,512]{1,0:T(8,128)(2,1)S(1)} collective-permute-done((bf16[512,512]{1,0:T(8,128)(2,1)S(1)}, bf16[512,512]{1,0:T(8,128)(2,1)S(1)}, u32[]{:S(2)}, u32[]{:S(2)}) %collective-permute-start.20) | collective-permute-done | bytes 524320 | tf_op jit(solution)/shard_map/ppermute | solution.py:43
  135.9 5.0 %collective-permute-start.25 = (bf16[512,512]{1,0:T(8,128)(2,1)S(1)}, bf16[512,512]{1,0:T(8,128)(2,1)S(1)}, u32[]{:S(2)}, u32[]{:S(2)}) collective-permute-start(bf16[512,512]{1,0:T(8,128)(2,1)S(1)} %mix.3.refs_1_), channel_id=1, source_target_pairs={{0,1},{1,0},{2,3},{3,2},{4,5},{5,4},{6,7},{7,6},{8,9},{9,8},{10,11... | collective-permute-start | bytes 1572872 | tf_op jit(solution)/shard_map/ppermute | solution.py:49
  140.9 3.0 %collective-permute-start.27 = (bf16[512,512]{1,0:T(8,128)(2,1)S(1)}, bf16[512,512]{1,0:T(8,128)(2,1)}, u32[]{:S(2)}, u32[]{:S(2)}) collective-permute-start(bf16[512,512]{1,0:T(8,128)(2,1)S(1)} %collective-permute-done.20.refs_4_), channel_id=1, source_target_pairs={{0,1},{1,0},{2,3},{3,2},{4,5},{5,4},{6,7},{7,6},{8,9},{9,8},{10,11... | collective-permute-start | bytes 1572872 | tf_op jit(solution)/shard_map/ppermute | solution.py:49
  143.9 3.3 %collective-permute-done.26.refs_5_ = bf16[512,512]{1,0:T(8,128)(2,1)} collective-permute-done((bf16[512,512]{1,0:T(8,128)(2,1)S(1)}, bf16[512,512]{1,0:T(8,128)(2,1)}, u32[]{:S(2)}, u32[]{:S(2)}) %collective-permute-start.26) | collective-permute-done | bytes 524320 | tf_op jit(solution)/shard_map/ppermute | solution.py:43
  147.1 2.7 %collective-permute-start.28 = (bf16[512,512]{1,0:T(8,128)(2,1)}, bf16[512,512]{1,0:T(8,128)(2,1)}, u32[]{:S(2)}, u32[]{:S(2)}) collective-permute-start(bf16[512,512]{1,0:T(8,128)(2,1)} %collective-permute-done.26.refs_5_), channel_id=1, source_target_pairs={{0,1},{1,0},{2,3},{3,2},{4,5},{5,4},{6,7},{7,6},{8,9},{9,8},{10,11... | collective-permute-start | bytes 1572872 | tf_op jit(solution)/shard_map/ppermute | solution.py:49
  149.9 1.1 collective-permute-start.30
  152.0 3.5 %collective-permute-start.23 = (bf16[512,512]{1,0:T(8,128)(2,1)S(1)}, bf16[512,512]{1,0:T(8,128)(2,1)S(1)}, u32[]{:S(2)}, u32[]{:S(2)}) collective-permute-start(bf16[512,512]{1,0:T(8,128)(2,1)S(1)} %collective-permute-done.22.refs_9_), channel_id=1, source_target_pairs={{0,6},{1,7},{2,0},{3,1},{4,2},{5,3},{6,4},{7,5},{8,14},{9,15},{10,... | collective-permute-start | bytes 1572872 | tf_op jit(solution)/shard_map/ppermute | solution.py:43
  156.2 8.9 %out.1 = (f32[1024,512]{1,0:T(8,128)}, bf16[2,512,512]{2,1,0:T(8,128)(2,1)}) custom-call(s32[12]{0:T(128)} %stack.99.order, bf16[512,512]{1,0:T(8,128)(2,1)} %copy-done.4, bf16[512,512]{1,0:T(8,128)(2,1)} %copy-done.5, bf16[512,512]{1,0:T(8,128)(2,1)} %copy-done.10, bf16[512,512]{1,0:T(8,128)(2,1)} %copy-done.11, bf16[512,512]{1,0:T(8,128)(2,1)} %copy-done.8, ...), custom_call_target="tpu_custom_call" | custom-call | flops 3221225472 | bytes 16777216 | tf_op jit(solution)/shard_map/out/pallas_call | solution.py:311
  165.2 1.4 collective-permute-done.21.mixed_0
  166.6 1.0 collective-permute-start.32
  167.7 1.2 copy-done.2
  168.9 1.6 copy-done.3
  171.2 1.7 add.229
  (95 shorter events, 8.1 us)
Async XLA Ops:
  6.5 31.4 %copy-start.12 = (bf16[512,128]{1,0:T(8,128)(2,1)S(1)}, bf16[512,128]{1,0:T(8,128)(2,1)}, u32[]{:S(2)}) copy-start(bf16[512,128]{1,0:T(8,128)(2,1)} %param.14) | copy-start | bytes 393220
  6.5 89.8 %all-gather.5.cloned.1.call-start = ((), (), s32[]{:S(2)}) async-start(), calls=%async_computation | async-start | bytes 4718592 | tf_op jit(solution)/shard_map/all_gather | solution.py:39
  6.5 14.7 %collective-permute-start = (bf16[128,512]{1,0:T(8,128)(2,1)}, bf16[128,512]{1,0:T(8,128)(2,1)S(1)}, u32[]{:S(2)}, u32[]{:S(2)}) collective-permute-start(bf16[128,512]{1,0:T(8,128)(2,1)} %param.11), channel_id=1, source_target_pairs={{0,64},{8,72},{16,80},{24,88},{32,96},{40,104},{48,112},{56,120},{... | collective-permute-start | bytes 393224 | tf_op jit(solution)/shard_map/ppermute | solution.py:33
  8.7 12.5 %collective-permute-start.1 = (bf16[128,512]{1,0:T(8,128)(2,1)}, bf16[128,512]{1,0:T(8,128)(2,1)S(1)}, u32[]{:S(2)}, u32[]{:S(2)}) collective-permute-start(bf16[128,512]{1,0:T(8,128)(2,1)} %param.11), channel_id=1, source_target_pairs={{0,128},{8,136},{16,144},{24,152},{32,160},{40,168},{48,176},{56,1... | collective-permute-start | bytes 393224 | tf_op jit(solution)/shard_map/ppermute | solution.py:33
  11.3 9.9 %collective-permute-start.2 = (bf16[128,512]{1,0:T(8,128)(2,1)}, bf16[128,512]{1,0:T(8,128)(2,1)S(1)}, u32[]{:S(2)}, u32[]{:S(2)}) collective-permute-start(bf16[128,512]{1,0:T(8,128)(2,1)} %param.11), channel_id=1, source_target_pairs={{0,192},{8,200},{16,208},{24,216},{32,224},{40,232},{48,240},{56,2... | collective-permute-start | bytes 393224 | tf_op jit(solution)/shard_map/ppermute | solution.py:33
  13.9 7.3 %collective-permute-start.3 = (bf16[128,256]{1,0:T(8,128)(2,1)S(1)}, bf16[128,256]{1,0:T(8,128)(2,1)S(1)}, u32[]{:S(2)}, u32[]{:S(2)}) collective-permute-start(bf16[128,256]{1,0:T(8,128)(2,1)S(1)} %constant_dynamic-update-slice_fusion), channel_id=1, source_target_pairs={{0,8},{8,16},{16,24},{24,32},{32,40},{40,48},{48,56},{56,0},{64,72... | collective-permute-start | bytes 196616 | tf_op jit(solution)/shard_map/ppermute | solution.py:23
  15.6 5.6 %collective-permute-start.4 = (bf16[128,256]{1,0:T(8,128)(2,1)S(1)}, bf16[128,256]{1,0:T(8,128)(2,1)S(1)}, u32[]{:S(2)}, u32[]{:S(2)}) collective-permute-start(bf16[128,256]{1,0:T(8,128)(2,1)S(1)} %constant_dynamic-update-slice_fusion), channel_id=1, source_target_pairs={{0,56},{8,0},{16,8},{24,16},{32,24},{40,32},{48,40},{56,48},{64,12... | collective-permute-start | bytes 196616 | tf_op jit(solution)/shard_map/ppermute | solution.py:23
  21.2 13.3 %collective-permute-start.5 = (bf16[3,128,256]{2,1,0:T(8,128)(2,1)S(1)}, bf16[3,128,256]{2,1,0:T(8,128)(2,1)S(1)}, u32[]{:S(2)}, u32[]{:S(2)}) collective-permute-start(bf16[3,128,256]{2,1,0:T(8,128)(2,1)S(1)} %pad_maximum_fusion.2), channel_id=1, source_target_pairs={{0,24},{8,32},{16,40},{24,48},{32,56},{40,0},{48,8},{56,16},{64,88... | collective-permute-start | bytes 589832 | tf_op jit(solution)/shard_map/ppermute | solution.py:23
  25.6 6.9 %collective-permute-start.6 = (bf16[2,128,256]{2,1,0:T(8,128)(2,1)S(1)}, bf16[2,128,256]{2,1,0:T(8,128)(2,1)S(1)}, u32[]{:S(2)}, u32[]{:S(2)}) collective-permute-start(bf16[2,128,256]{2,1,0:T(8,128)(2,1)S(1)} %pad_maximum_fusion.3), channel_id=1, source_target_pairs={{0,40},{8,48},{16,56},{24,0},{32,8},{40,16},{48,24},{56,32},{64,10... | collective-permute-start | bytes 393224 | tf_op jit(solution)/shard_map/ppermute | solution.py:23
  34.5 121.6 %all-gather.7.cloned.1.call-start = ((), (), s32[]{:S(2)}) async-start(), calls=%async_computation.1 | async-start | bytes 4718592 | tf_op jit(solution)/shard_map/all_gather | solution.py:39
  34.9 24.4 %collective-permute-start.7 = (bf16[8,128,256]{2,1,0:T(8,128)(2,1)S(1)}, bf16[8,128,256]{2,1,0:T(8,128)(2,1)S(1)}, u32[]{:S(2)}, u32[]{:S(2)}) collective-permute-start(bf16[8,128,256]{2,1,0:T(8,128)(2,1)S(1)} %constant_dynamic-slice_fusion.refs_4_), channel_id=1, source_target_pairs={{0,64},{8,72},{16,80},{24,88},{32,96},{40,104},{48,112},{56,120},{... | collective-permute-start | bytes 1572872 | tf_op jit(solution)/shard_map/ppermute | solution.py:33
  35.4 23.9 %collective-permute-start.8 = (bf16[8,128,256]{2,1,0:T(8,128)(2,1)S(1)}, bf16[8,128,256]{2,1,0:T(8,128)(2,1)S(1)}, u32[]{:S(2)}, u32[]{:S(2)}) collective-permute-start(bf16[8,128,256]{2,1,0:T(8,128)(2,1)S(1)} %constant_dynamic-slice_fusion.refs_4_), channel_id=1, source_target_pairs={{0,128},{8,136},{16,144},{24,152},{32,160},{40,168},{48,176},{56,1... | collective-permute-start | bytes 1572872 | tf_op jit(solution)/shard_map/ppermute | solution.py:33
  35.4 28.1 %collective-permute-start.9 = (bf16[8,128,256]{2,1,0:T(8,128)(2,1)S(1)}, bf16[8,128,256]{2,1,0:T(8,128)(2,1)S(1)}, u32[]{:S(2)}, u32[]{:S(2)}) collective-permute-start(bf16[8,128,256]{2,1,0:T(8,128)(2,1)S(1)} %constant_dynamic-slice_fusion.refs_4_), channel_id=1, source_target_pairs={{0,192},{8,200},{16,208},{24,216},{32,224},{40,232},{48,240},{56,2... | collective-permute-start | bytes 1572872 | tf_op jit(solution)/shard_map/ppermute | solution.py:33
  37.9 20.2 %collective-permute-start.10 = (bf16[512,128]{1,0:T(8,128)(2,1)S(1)}, bf16[512,128]{1,0:T(8,128)(2,1)S(1)}, u32[]{:S(2)}, u32[]{:S(2)}) collective-permute-start(bf16[512,128]{1,0:T(8,128)(2,1)S(1)} %copy-done.12), channel_id=1, source_target_pairs={{0,0},{32,1},{64,2},{96,3},{128,4},{160,5},{192,6},{224,7},{1,8},{... | collective-permute-start | bytes 393224 | tf_op jit(solution)/shard_map/ppermute | solution.py:58
  46.6 46.5 %copy-start.13 = (f32[4]{0:T(128)S(1)}, f32[4]{0:T(128)}, u32[]{:S(2)}) copy-start(f32[4]{0:T(128)} %param.15) | copy-start | bytes 52
  63.6 13.0 %collective-permute-start.11 = (bf16[512,128]{1,0:T(8,128)(2,1)S(1)}, bf16[512,128]{1,0:T(8,128)(2,1)S(1)}, u32[]{:S(2)}, u32[]{:S(2)}) collective-permute-start(bf16[512,128]{1,0:T(8,128)(2,1)S(1)} %collective-permute-done.10), channel_id=1, source_target_pairs={{0,64},{8,72},{16,80},{24,88},{32,96},{40,104},{48,112},{56,120},{... | collective-permute-start | bytes 393224 | tf_op jit(solution)/shard_map/ppermute | solution.py:33
  63.6 13.0 %collective-permute-start.12 = (bf16[512,128]{1,0:T(8,128)(2,1)S(1)}, bf16[512,128]{1,0:T(8,128)(2,1)S(1)}, u32[]{:S(2)}, u32[]{:S(2)}) collective-permute-start(bf16[512,128]{1,0:T(8,128)(2,1)S(1)} %collective-permute-done.10), channel_id=1, source_target_pairs={{0,128},{8,136},{16,144},{24,152},{32,160},{40,168},{48,176},{56,1... | collective-permute-start | bytes 393224 | tf_op jit(solution)/shard_map/ppermute | solution.py:33
  68.3 8.3 %collective-permute-start.13 = (bf16[512,128]{1,0:T(8,128)(2,1)S(1)}, bf16[512,128]{1,0:T(8,128)(2,1)S(1)}, u32[]{:S(2)}, u32[]{:S(2)}) collective-permute-start(bf16[512,128]{1,0:T(8,128)(2,1)S(1)} %collective-permute-done.10), channel_id=1, source_target_pairs={{0,192},{8,200},{16,208},{24,216},{32,224},{40,232},{48,240},{56,2... | collective-permute-start | bytes 393224 | tf_op jit(solution)/shard_map/ppermute | solution.py:33
  68.3 3.4 %copy-start = (bf16[1024,4096]{1,0:T(8,128)(2,1)S(1)}, bf16[1024,4096]{1,0:T(8,128)(2,1)}, u32[]{:S(2)}) copy-start(bf16[1024,4096]{1,0:T(8,128)(2,1)} %norm.1.refs_0_.refs_1_.refs_2_.refs_3_) | copy-start | bytes 25165828
  77.5 4.0 %collective-permute-start.14 = (bf16[136,128]{1,0:T(8,128)(2,1)S(1)}, bf16[136,128]{1,0:T(8,128)(2,1)S(1)}, u32[]{:S(2)}, u32[]{:S(2)}) collective-permute-start(bf16[136,128]{1,0:T(8,128)(2,1)S(1)} %get-tuple-element.75), channel_id=1, source_target_pairs={{0,8},{8,0},{16,24},{24,16},{32,40},{40,32},{48,56},{56,48},{64,72... | collective-permute-start | bytes 104456 | tf_op jit(solution)/shard_map/ppermute | solution.py:29
  81.5 6.6 %collective-permute-start.15 = (bf16[136,128]{1,0:T(8,128)(2,1)S(1)}, bf16[136,128]{1,0:T(8,128)(2,1)S(1)}, u32[]{:S(2)}, u32[]{:S(2)}) collective-permute-start(bf16[136,128]{1,0:T(8,128)(2,1)S(1)} %fusion.6), channel_id=1, source_target_pairs={{0,16},{8,24},{16,0},{24,8},{32,48},{40,56},{48,32},{56,40},{64,80... | collective-permute-start | bytes 104456 | tf_op jit(solution)/shard_map/ppermute | solution.py:29
  88.1 7.6 %collective-permute-start.16 = (bf16[136,128]{1,0:T(8,128)(2,1)S(1)}, bf16[136,128]{1,0:T(8,128)(2,1)S(1)}, u32[]{:S(2)}, u32[]{:S(2)}) collective-permute-start(bf16[136,128]{1,0:T(8,128)(2,1)S(1)} %fusion.7), channel_id=1, source_target_pairs={{0,32},{8,40},{16,48},{24,56},{32,0},{40,8},{48,16},{56,24},{64,96... | collective-permute-start | bytes 104456 | tf_op jit(solution)/shard_map/ppermute | solution.py:29
  96.4 24.8 %collective-permute-start.19 = (bf16[136,128]{1,0:T(8,128)(2,1)S(1)}, bf16[136,128]{1,0:T(8,128)(2,1)S(1)}, u32[]{:S(2)}, u32[]{:S(2)}) collective-permute-start(bf16[136,128]{1,0:T(8,128)(2,1)S(1)} %convert_add_fusion), channel_id=1, source_target_pairs={{0,192},{8,200},{16,208},{24,216},{32,224},{40,232},{48,240},{56,2... | collective-permute-start | bytes 104456 | tf_op jit(solution)/shard_map/ppermute | solution.py:33
  100.8 20.4 %collective-permute-start.18 = (bf16[136,128]{1,0:T(8,128)(2,1)S(1)}, bf16[136,128]{1,0:T(8,128)(2,1)S(1)}, u32[]{:S(2)}, u32[]{:S(2)}) collective-permute-start(bf16[136,128]{1,0:T(8,128)(2,1)S(1)} %convert_add_fusion), channel_id=1, source_target_pairs={{0,128},{8,136},{16,144},{24,152},{32,160},{40,168},{48,176},{56,1... | collective-permute-start | bytes 104456 | tf_op jit(solution)/shard_map/ppermute | solution.py:33
  102.2 18.9 %collective-permute-start.17 = (bf16[136,128]{1,0:T(8,128)(2,1)S(1)}, bf16[136,128]{1,0:T(8,128)(2,1)S(1)}, u32[]{:S(2)}, u32[]{:S(2)}) collective-permute-start(bf16[136,128]{1,0:T(8,128)(2,1)S(1)} %convert_add_fusion), channel_id=1, source_target_pairs={{0,64},{8,72},{16,80},{24,88},{32,96},{40,104},{48,112},{56,120},{... | collective-permute-start | bytes 104456 | tf_op jit(solution)/shard_map/ppermute | solution.py:33
  103.1 18.1 %copy-start.6 = (f32[1,128,128]{2,1,0:T(8,128)S(1)}, f32[1,128,128]{2,1,0:T(8,128)}, u32[]{:S(2)}) copy-start(f32[1,128,128]{2,1,0:T(8,128)} %param.16) | copy-start | bytes 196612
  113.0 8.1 %copy-start.7 = (f32[1,128]{1,0:T(1,128)S(1)}, f32[1,128]{1,0:T(1,128)}, u32[]{:S(2)}) copy-start(f32[1,128]{1,0:T(1,128)} %param.17) | copy-start | bytes 1540
  113.0 1.2 copy-start.1
  122.9 33.3 %copy-start.4 = (bf16[512,512]{1,0:T(8,128)(2,1)}, bf16[512,512]{1,0:T(8,128)(2,1)S(1)}, u32[]{:S(2)}) copy-start(bf16[512,512]{1,0:T(8,128)(2,1)S(1)} %mix.2.refs_0_) | copy-start | bytes 1572868
  122.9 13.0 %collective-permute-start.20 = (bf16[512,512]{1,0:T(8,128)(2,1)S(1)}, bf16[512,512]{1,0:T(8,128)(2,1)S(1)}, u32[]{:S(2)}, u32[]{:S(2)}) collective-permute-start(bf16[512,512]{1,0:T(8,128)(2,1)S(1)} %mix.2.refs_0_), channel_id=1, source_target_pairs={{0,2},{1,3},{2,4},{3,5},{4,6},{5,7},{6,0},{7,1},{8,10},{9,11},{10,... | collective-permute-start | bytes 1572872 | tf_op jit(solution)/shard_map/ppermute | solution.py:43
  124.7 31.5 %copy-start.5 = (bf16[512,512]{1,0:T(8,128)(2,1)}, bf16[512,512]{1,0:T(8,128)(2,1)S(1)}, u32[]{:S(2)}) copy-start(bf16[512,512]{1,0:T(8,128)(2,1)S(1)} %mix.3.refs_1_) | copy-start | bytes 1572868
  124.7 16.2 %collective-permute-start.22 = (bf16[512,512]{1,0:T(8,128)(2,1)S(1)}, bf16[512,512]{1,0:T(8,128)(2,1)S(1)}, u32[]{:S(2)}, u32[]{:S(2)}) collective-permute-start(bf16[512,512]{1,0:T(8,128)(2,1)S(1)} %mix.3.refs_1_), channel_id=1, source_target_pairs={{0,6},{1,7},{2,0},{3,1},{4,2},{5,3},{6,4},{7,5},{8,14},{9,15},{10,... | collective-permute-start | bytes 1572872 | tf_op jit(solution)/shard_map/ppermute | solution.py:43
  127.6 19.5 %collective-permute-start.26 = (bf16[512,512]{1,0:T(8,128)(2,1)S(1)}, bf16[512,512]{1,0:T(8,128)(2,1)}, u32[]{:S(2)}, u32[]{:S(2)}) collective-permute-start(bf16[512,512]{1,0:T(8,128)(2,1)S(1)} %mix.3.refs_1_), channel_id=1, source_target_pairs={{0,2},{1,3},{2,4},{3,5},{4,6},{5,7},{6,0},{7,1},{8,10},{9,11},{10,... | collective-permute-start | bytes 1572872 | tf_op jit(solution)/shard_map/ppermute | solution.py:43
  127.6 22.3 %collective-permute-start.29 = (bf16[512,512]{1,0:T(8,128)(2,1)S(1)}, bf16[512,512]{1,0:T(8,128)(2,1)}, u32[]{:S(2)}, u32[]{:S(2)}) collective-permute-start(bf16[512,512]{1,0:T(8,128)(2,1)S(1)} %mix.2.refs_0_), channel_id=1, source_target_pairs={{0,6},{1,7},{2,0},{3,1},{4,2},{5,3},{6,4},{7,5},{8,14},{9,15},{10,... | collective-permute-start | bytes 1572872 | tf_op jit(solution)/shard_map/ppermute | solution.py:43
  130.3 20.7 %collective-permute-start.24 = (bf16[512,512]{1,0:T(8,128)(2,1)S(1)}, bf16[512,512]{1,0:T(8,128)(2,1)S(1)}, u32[]{:S(2)}, u32[]{:S(2)}) collective-permute-start(bf16[512,512]{1,0:T(8,128)(2,1)S(1)} %mix.2.refs_0_), channel_id=1, source_target_pairs={{0,1},{1,0},{2,3},{3,2},{4,5},{5,4},{6,7},{7,6},{8,9},{9,8},{10,11... | collective-permute-start | bytes 1572872 | tf_op jit(solution)/shard_map/ppermute | solution.py:49
  135.9 20.3 %copy-start.8 = (bf16[512,512]{1,0:T(8,128)(2,1)}, bf16[512,512]{1,0:T(8,128)(2,1)S(1)}, u32[]{:S(2)}) copy-start(bf16[512,512]{1,0:T(8,128)(2,1)S(1)} %collective-permute-done.20.refs_4_) | copy-start | bytes 1572868
  135.9 15.2 %collective-permute-start.25 = (bf16[512,512]{1,0:T(8,128)(2,1)S(1)}, bf16[512,512]{1,0:T(8,128)(2,1)S(1)}, u32[]{:S(2)}, u32[]{:S(2)}) collective-permute-start(bf16[512,512]{1,0:T(8,128)(2,1)S(1)} %mix.3.refs_1_), channel_id=1, source_target_pairs={{0,1},{1,0},{2,3},{3,2},{4,5},{5,4},{6,7},{7,6},{8,9},{9,8},{10,11... | collective-permute-start | bytes 1572872 | tf_op jit(solution)/shard_map/ppermute | solution.py:49
  140.9 15.3 %copy-start.9 = (bf16[512,512]{1,0:T(8,128)(2,1)}, bf16[512,512]{1,0:T(8,128)(2,1)S(1)}, u32[]{:S(2)}) copy-start(bf16[512,512]{1,0:T(8,128)(2,1)S(1)} %collective-permute-done.22.refs_9_) | copy-start | bytes 1572868
  140.9 10.2 %collective-permute-start.27 = (bf16[512,512]{1,0:T(8,128)(2,1)S(1)}, bf16[512,512]{1,0:T(8,128)(2,1)}, u32[]{:S(2)}, u32[]{:S(2)}) collective-permute-start(bf16[512,512]{1,0:T(8,128)(2,1)S(1)} %collective-permute-done.20.refs_4_), channel_id=1, source_target_pairs={{0,1},{1,0},{2,3},{3,2},{4,5},{5,4},{6,7},{7,6},{8,9},{9,8},{10,11... | collective-permute-start | bytes 1572872 | tf_op jit(solution)/shard_map/ppermute | solution.py:49
  147.1 9.0 %collective-permute-start.28 = (bf16[512,512]{1,0:T(8,128)(2,1)}, bf16[512,512]{1,0:T(8,128)(2,1)}, u32[]{:S(2)}, u32[]{:S(2)}) collective-permute-start(bf16[512,512]{1,0:T(8,128)(2,1)} %collective-permute-done.26.refs_5_), channel_id=1, source_target_pairs={{0,1},{1,0},{2,3},{3,2},{4,5},{5,4},{6,7},{7,6},{8,9},{9,8},{10,11... | collective-permute-start | bytes 1572872 | tf_op jit(solution)/shard_map/ppermute | solution.py:49
  149.9 6.3 %collective-permute-start.30 = (bf16[512,512]{1,0:T(8,128)(2,1)}, bf16[512,512]{1,0:T(8,128)(2,1)}, u32[]{:S(2)}, u32[]{:S(2)}) collective-permute-start(bf16[512,512]{1,0:T(8,128)(2,1)} %collective-permute-done.29.refs_8_), channel_id=1, source_target_pairs={{0,1},{1,0},{2,3},{3,2},{4,5},{5,4},{6,7},{7,6},{8,9},{9,8},{10,11... | collective-permute-start | bytes 1572872 | tf_op jit(solution)/shard_map/ppermute | solution.py:49
  151.0 5.2 %collective-permute-start.31 = (bf16[512,512]{1,0:T(8,128)(2,1)S(1)}, bf16[512,512]{1,0:T(8,128)(2,1)}, u32[]{:S(2)}, u32[]{:S(2)}) collective-permute-start(bf16[512,512]{1,0:T(8,128)(2,1)S(1)} %collective-permute-done.22.refs_9_), channel_id=1, source_target_pairs={{0,1},{1,0},{2,3},{3,2},{4,5},{5,4},{6,7},{7,6},{8,9},{9,8},{10,11... | collective-permute-start | bytes 1572872 | tf_op jit(solution)/shard_map/ppermute | solution.py:49
  151.1 15.5 %collective-permute-start.21 = (bf16[512,512]{1,0:T(8,128)(2,1)S(1)}, bf16[512,512]{1,0:T(8,128)(2,1)S(1)}, u32[]{:S(2)}, u32[]{:S(2)}) collective-permute-start(bf16[512,512]{1,0:T(8,128)(2,1)S(1)} %collective-permute-done.20.refs_4_), channel_id=1, source_target_pairs={{0,2},{1,3},{2,4},{3,5},{4,6},{5,7},{6,0},{7,1},{8,10},{9,11},{10,... | collective-permute-start | bytes 1572872 | tf_op jit(solution)/shard_map/ppermute | solution.py:43
  152.0 14.6 %collective-permute-start.23 = (bf16[512,512]{1,0:T(8,128)(2,1)S(1)}, bf16[512,512]{1,0:T(8,128)(2,1)S(1)}, u32[]{:S(2)}, u32[]{:S(2)}) collective-permute-start(bf16[512,512]{1,0:T(8,128)(2,1)S(1)} %collective-permute-done.22.refs_9_), channel_id=1, source_target_pairs={{0,6},{1,7},{2,0},{3,1},{4,2},{5,3},{6,4},{7,5},{8,14},{9,15},{10,... | collective-permute-start | bytes 1572872 | tf_op jit(solution)/shard_map/ppermute | solution.py:43
  166.6 4.6 %collective-permute-start.32 = (bf16[512,512]{1,0:T(8,128)(2,1)S(1)}, bf16[512,512]{1,0:T(8,128)(2,1)S(1)}, u32[]{:S(2)}, u32[]{:S(2)}) collective-permute-start(bf16[512,512]{1,0:T(8,128)(2,1)S(1)} %collective-permute-done.21.mixed_0), channel_id=1, source_target_pairs={{0,1},{1,0},{2,3},{3,2},{4,5},{5,4},{6,7},{7,6},{8,9},{9,8},{10,11... | collective-permute-start | bytes 1572872 | tf_op jit(solution)/shard_map/ppermute | solution.py:49
  167.6 3.5 %collective-permute-start.33 = (bf16[512,512]{1,0:T(8,128)(2,1)S(1)}, bf16[512,512]{1,0:T(8,128)(2,1)S(1)}, u32[]{:S(2)}, u32[]{:S(2)}) collective-permute-start(bf16[512,512]{1,0:T(8,128)(2,1)S(1)} %collective-permute-done.23.mixed_1), channel_id=1, source_target_pairs={{0,1},{1,0},{2,3},{3,2},{4,5},{5,4},{6,7},{7,6},{8,9},{9,8},{10,11... | collective-permute-start | bytes 1572872 | tf_op jit(solution)/shard_map/ppermute | solution.py:49
  167.7 1.2 copy-start.2
  168.9 1.6 copy-start.3
  (2 other events, 1.7 us)
Sparse Core Ops, SparseCore 0:
  34.7 61.6 all-gather.4
  98.1 56.0 all-gather.6
